TPU v7x, 256 devices: a whole 4x4x8 slice. The times are simulated.
256 devices in a mesh: elem: 64 (over y, z, core), snap: 4 (over x).
Axes of the slice: x: 4, y: 4, z: 8, core: 2. Of those that a mesh axis runs over, the one named last changes fastest.
Arguments:
- node_basis: bfloat16 [65536, 1536], P('elem'), may hold values from -0.25 to 0.25
- stiff_terms: bfloat16 [16, 24, 24], replicated, may hold values from -1.25 to 1.25
- reduced_coords: bfloat16 [512, 32], P(None, 'snap'), may hold values from -6 to 6
- sample_list: int32 [512], replicated, may hold values from 0 to 2047, as said below
- connectivity: int32 [2048, 8], replicated, may hold values from -1 to 65535, as said below
- node_slot: int32 [65536], replicated, may hold values from 0 to 65535, as said below
- elem_device: int32 [512], replicated, may hold values from 0 to 63, as said below
Outputs:
- ortho_panel: float32 [1024, 512, 512], P('elem', 'snap')
- triangle_factor: float32 [512, 512], P('elem')
Inputs may be any that keep to these rules, and one draw needn't show every extreme that they name: `sample_list`: distinct element ids. `connectivity`: each element lists 4, 6 or 8 live nodes first and -1 after them; the live nodes of one element are owned by distinct indices of elem (owner = node_slot // 1024); for every index d of elem and every owner o, at most 2 sampled elements computed on d have a live node owned by o, and some pair (d, o) reaches 2. `node_slot`: a permutation. `elem_device`: each index of elem computes at most 16 sampled elements; some index computes exactly 16.
All inputs are finite; a program needn't handle non-finite values.
Results may differ from a plain program's by a relative error of at most 0.0056.
Values may be sent and summed in bfloat16 or wider, within the bound.
A program may use at most 64 MiB of HBM per device.

v0:
```python
import jax
import jax.numpy as jnp
from jax import lax
from jax.sharding import PartitionSpec as P

MODES = 512
ENODES = 8
NDOF = 3


def shards(
    node_basis, stiff_terms, reduced_coords, sample_list, connectivity, node_slot, elem_device
):
    devices = lax.axis_size("elem")
    elem_rank = lax.axis_index("elem")
    node_rows = node_basis.shape[0]
    sampled = sample_list.shape[0]
    capacity = 2 * sampled // devices
    pair_bound = (capacity * ENODES + devices - 1) // devices
    node_ids = connectivity[sample_list]
    live_nodes = node_ids >= 0
    stored_rows = jnp.where(live_nodes, node_slot[jnp.maximum(node_ids, 0)], 0)
    owners = stored_rows // node_rows
    local_rows = stored_rows % node_rows
    position_ids = jnp.arange(sampled, dtype=jnp.int32)
    earlier = position_ids[None, :] < position_ids[:, None]
    same_device = elem_device[None, :] == elem_device[:, None]
    in_group = earlier & same_device
    slot_ids = jnp.sum(in_group.astype(jnp.int32), axis=1)
    owner_ids = jnp.arange(devices, dtype=jnp.int32)
    owned_mask = jnp.any(live_nodes[:, :, None] & (owners[:, :, None] == owner_ids), axis=1).astype(
        jnp.float32
    )
    ranks_by_owner = jnp.dot(
        in_group.astype(jnp.float32), owned_mask, precision=lax.Precision.HIGHEST
    ).astype(jnp.int32)
    peer_ranks = jnp.take_along_axis(ranks_by_owner, owners, axis=1)
    sending = live_nodes & (owners == elem_rank)
    target = jnp.where(sending, elem_device[:, None], devices)
    row_table = (
        jnp.full((devices, pair_bound), -1, jnp.int32)
        .at[target, peer_ranks]
        .set(local_rows, mode="drop")
    )
    send_rows = node_basis[jnp.maximum(row_table, 0)]
    outgoing = jnp.where((row_table >= 0)[:, :, None], send_rows, jnp.zeros((), jnp.bfloat16))
    incoming = lax.all_to_all(outgoing, "elem", split_axis=0, concat_axis=0, tiled=True)
    at_device = elem_device == elem_rank
    slot_index = jnp.where(at_device, slot_ids, capacity)
    slot_elem = (
        jnp.full((capacity,), sampled, jnp.int32).at[slot_index].set(position_ids, mode="drop")
    )
    slot_live = slot_elem < sampled
    picked = jnp.minimum(slot_elem, sampled - 1)
    slot_rows = incoming[owners[picked], jnp.minimum(peer_ranks[picked], pair_bound - 1)]
    slot_mask = live_nodes[picked] & slot_live[:, None]
    local_basis = jnp.where(slot_mask[:, :, None], slot_rows, jnp.zeros((), jnp.bfloat16))
    element_basis = local_basis.reshape(capacity, ENODES * NDOF, MODES)
    displaced = jnp.einsum(
        "ekm,ms->eks", element_basis, reduced_coords, preferred_element_type=jnp.float32
    ).astype(jnp.bfloat16)
    forces = jnp.einsum(
        "tkl,els->ekst", stiff_terms, displaced, preferred_element_type=jnp.float32
    ).astype(jnp.bfloat16)
    forces = forces.reshape(capacity, ENODES * NDOF, -1)
    projected = jnp.einsum(
        "ekm,ekc->emc", element_basis, forces, preferred_element_type=jnp.float32
    ).astype(jnp.bfloat16)
    banded = lax.all_to_all(projected, "snap", split_axis=1, concat_axis=2, tiled=True)
    band_rows = banded.reshape(-1, banded.shape[2])
    columns = band_rows.shape[1]
    total_rows = sampled * MODES
    partial_gram = lax.dot_general(
        band_rows, band_rows, (((0,), (0,)), ((), ())), preferred_element_type=jnp.float32
    )
    gram_matrix = lax.psum(partial_gram, ("elem", "snap"))
    gram_matrix = gram_matrix / total_rows
    lower_factor = jnp.linalg.cholesky(gram_matrix)
    identity_matrix = jnp.eye(columns, dtype=jnp.float32)
    lower_inverse = jax.scipy.linalg.solve_triangular(lower_factor, identity_matrix, lower=True)
    ortho_rows = lax.dot_general(
        band_rows.astype(jnp.float32),
        lower_inverse,
        (((1,), (1,)), ((), ())),
        precision=lax.Precision.HIGHEST,
        preferred_element_type=jnp.float32,
    )
    share = columns // devices
    upper_rows = lax.dynamic_slice_in_dim(lower_factor.T, elem_rank * share, share, 0)
    return (ortho_rows.reshape(banded.shape), upper_rows)


def solution(mesh):
    placed = (P("elem", None), P(), P(None, "snap"), P(), P(), P(), P())
    return jax.shard_map(
        shards,
        mesh=mesh,
        in_specs=placed,
        out_specs=(P("elem", "snap", None), P("elem", None)),
        check_vma=False,
    )
```

profile of v0, /device:TPU:1, one launch (start us, length us, event | category | flops | bytes accessed | tf_op | source)
XLA Modules:
  0.0 629.8 jit_solution(7660797386319666554)
XLA Ops:
  10.3 2.9 gather_fusion
  15.9 23.0 %gather_fusion.2 = s32[4096]{0:T(1024)S(1)} fusion(s32[65536]{0:T(1024)S(1)} %copy-done.1, s32[4096]{0:T(1024)S(1)} %broadcast_clamp_fusion), kind=kCustom, calls=%fused_computation.2 | custom fusion | bytes 49152 | tf_op jit(solution)/shard_map/gather | solution.py:22
  48.0 33.0 %gather_fusion.7 = s32[4096]{0:T(1024)S(1)} fusion(s32[512,64]{0,1:T(8,128)S(1)} %convolution_convert_fusion.2, s32[4096]{0:T(1024)S(1)} %reshape.363), kind=kCustom, calls=%fused_computation.7 | custom fusion | bytes 65536 | tf_op jit(solution)/shard_map/jit(take_along_axis)/gather | solution.py:37
  88.4 15.5 %scatter_custom_fusion.1 = s32[128]{0:T(128)S(1)} fusion(s32[4096]{0:T(1024)S(1)} %reshape.377, s32[4096]{0:T(1024)S(1)} %reshape.379, s32[]{:T(128)} %constant.211.clone.1), kind=kCustom, calls=%fused_computation.155 | custom fusion | bytes 516
  109.7 13.1 %all-to-all-start = ((bf16[64,2,1536]{2,1,0:T(2,128)(2,1)}), bf16[64,2,1536]{2,1,0:T(2,128)(2,1)S(1)}, u32[]{:S(2)}, u32[]{:S(2)}) async-start(bf16[64,2,1536]{2,1,0:T(2,128)(2,1)} %broadcast_select_fusion), calls=%async_computation | async-start | bytes 786432 | tf_op jit(solution)/shard_map/all_to_all | solution.py:47
  125.8 3.5 scatter_custom_fusion
  152.4 29.3 %all_to_all.20 = bf16[16,512,128]{2,0,1:T(8,128)(2,1)} all-to-all(bf16[16,512,128]{2,0,1:T(8,128)(2,1)S(1)} %copy.125), channel_id=1, replica_groups=mesh['elem'=64,'snap'=4] {'snap'}, dimensions={1} | all-to-all | bytes 4194304 | tf_op jit(solution)/shard_map/all_to_all | solution.py:69
  181.7 5.1 copy.126
  186.8 4.5 fusion
  193.3 4.5 copy.127
  197.8 4.3 dot_general.24
  202.1 247.4 %all-reduce.3.cloned.1.call-done = f32[512,512]{0,1:T(8,128)} async-done(((f32[512,512]{0,1:T(8,128)}), f32[512,512]{0,1:T(8,128)}) %all-reduce.3.cloned.1.call-update) | async-done | bytes 1048592 | tf_op jit(solution)/shard_map/psum | solution.py:76
  457.1 11.7 %cholesky.104 = f32[128,128]{1,0:T(8,128)S(1)} custom-call(f32[128,128]{1,0:T(8,128)S(1)} %cholesky.266), custom_call_target="Cholesky" | custom-call | tf_op jit(solution)/shard_map/jit(cholesky)/cholesky | solution.py:78
  469.4 9.8 %custom-call.31 = f32[1,128,128]{1,2,0:T(8,128)S(1)} custom-call(f32[1,128,128]{2,1,0:T(8,128)S(1)} %get-tuple-element.47), custom_call_target="InvertDiagBlocksLowerTriangular" | custom-call | tf_op jit(solution)/shard_map/jit(cholesky)/cholesky | solution.py:78
  483.6 11.7 %cholesky.217 = f32[128,128]{1,0:T(8,128)S(1)} custom-call(f32[128,128]{1,0:T(8,128)S(1)} %cholesky.270), custom_call_target="Cholesky" | custom-call | tf_op jit(solution)/shard_map/jit(cholesky)/cholesky | solution.py:78
  498.7 10.0 %custom-call.32 = f32[1,128,128]{1,2,0:T(8,128)S(1)} custom-call(f32[1,128,128]{2,1,0:T(8,128)S(1)} %get-tuple-element.44), custom_call_target="InvertDiagBlocksLowerTriangular" | custom-call | tf_op jit(solution)/shard_map/jit(cholesky)/cholesky | solution.py:78
  512.0 11.7 %cholesky.238 = f32[128,128]{1,0:T(8,128)S(1)} custom-call(f32[128,128]{1,0:T(8,128)S(1)} %cholesky.275), custom_call_target="Cholesky" | custom-call | tf_op jit(solution)/shard_map/jit(cholesky)/cholesky | solution.py:78
  524.9 9.8 %custom-call.33 = f32[1,128,128]{1,2,0:T(8,128)S(1)} custom-call(f32[1,128,128]{2,1,0:T(8,128)S(1)} %get-tuple-element.41), custom_call_target="InvertDiagBlocksLowerTriangular" | custom-call | tf_op jit(solution)/shard_map/jit(cholesky)/cholesky | solution.py:78
  537.0 11.9 %cholesky.255 = f32[128,128]{1,0:T(8,128)S(1)} custom-call(f32[128,128]{1,0:T(8,128)S(1)} %convolution_subtract_fusion.5), custom_call_target="Cholesky" | custom-call | tf_op jit(solution)/shard_map/jit(cholesky)/cholesky | solution.py:78
  556.7 13.5 %while.1 = (s32[]{:T(128)}, f32[512,512]{1,0:T(8,128)}, s32[4,2]{0,1:T(2,128)S(1)}, f32[4,128,128]{2,1,0:T(8,128)}, s32[]{:T(128)}) while((s32[]{:T(128)}, f32[512,512]{1,0:T(8,128)}, s32[4,2]{0,1:T(2,128)S(1)}, f32[4,128,128]{2,1,0:T(8,128)}, s32[]{:T(128)}) %tuple.39), condition=%wide.while_cond, body=%wide.while_body.sunk | while | flops 2 | bytes 132205 | solution.py:80
  557.3 2.8 bitcast_dynamic-update-slice_fusion.2
  560.7 2.8 bitcast_dynamic-update-slice_fusion.2
  570.2 40.1 %custom-call.34 = f32[4,128,128]{1,2,0:T(8,128)S(1)} custom-call(f32[4,128,128]{2,1,0:T(8,128)} %get-tuple-element.9), custom_call_target="InvertDiagBlocksLowerTriangular" | custom-call | tf_op jit(solution)/shard_map/jit(_solve_triangular)/triangular_solve | solution.py:80
  617.4 5.1 fusion.4
  (137 shorter events, 98.7 us)
Async XLA Ops:
  7.2 97.9 %copy-start = (bf16[1024,1536]{1,0:T(8,128)(2,1)S(1)}, bf16[1024,1536]{1,0:T(8,128)(2,1)}, u32[]{:S(2)}) copy-start(bf16[1024,1536]{1,0:T(8,128)(2,1)} %param.7) | copy-start | bytes 9437188
  8.0 7.9 %copy-start.1 = (s32[65536]{0:T(1024)S(1)}, s32[65536]{0:T(1024)}, u32[]{:S(2)}) copy-start(s32[65536]{0:T(1024)} %param.12) | copy-start | bytes 786436
  39.0 8.6 %copy-start.8 = (s32[512]{0:T(512)S(1)}, s32[512]{0:T(512)}, u32[]{:S(2)}) copy-start(s32[512]{0:T(512)} %param.13) | copy-start | bytes 6148
  40.0 1.9 copy-start.5
  41.9 40.0 %copy-start.6 = (pred[512,8]{1,0:T(8,128)(4,1)}, pred[512,8]{1,0:T(8,128)(4,1)S(1)}, u32[]{:S(2)}) copy-start(pred[512,8]{1,0:T(8,128)(4,1)S(1)} %get-tuple-element.33) | copy-start | bytes 12292
  43.1 1.3 copy-start.4
  47.9 38.2 %copy-start.10 = (s32[2]{0:T(128)S(1)}, s32[2]{0:T(128)}, u32[]{:S(2)}) copy-start(s32[2]{0:T(128)} %constant.235) | copy-start | bytes 28
  48.0 38.2 %copy-start.9 = (s32[2]{0:T(128)S(1)}, s32[2]{0:T(128)}, u32[]{:S(2)}) copy-start(s32[2]{0:T(128)} %constant.232) | copy-start | bytes 28
  109.7 33.8 %all-to-all-start = ((bf16[64,2,1536]{2,1,0:T(2,128)(2,1)}), bf16[64,2,1536]{2,1,0:T(2,128)(2,1)S(1)}, u32[]{:S(2)}, u32[]{:S(2)}) async-start(bf16[64,2,1536]{2,1,0:T(2,128)(2,1)} %broadcast_select_fusion), calls=%async_computation | async-start | bytes 786432 | tf_op jit(solution)/shard_map/all_to_all | solution.py:47
  122.9 326.6 %all-reduce.3.cloned.1.call-start = ((), (), s32[]{:S(2)}) async-start(), calls=%async_computation.2 | async-start | bytes 2097152 | tf_op jit(solution)/shard_map/psum | solution.py:76
  456.1 1.0 copy-start.3
  468.8 0.6 copy-start.7
  612.8 4.6 copy-start.2
Sparse Core Ops, SparseCore 0:
  191.5 257.9 all-reduce.2
where the time goes:
time: 639 us; the launch traced here: 630 us
  waiting for transfers between devices  247 us (39%)
  other arithmetic  149 us (23%)
  local copies, waits for them, and re-layouts  144 us (23%)
  matrix products  29.9 us (5%)
  blocking collectives  29.3 us (5%)
  between operations  17.5 us (3%)
  starting transfers between devices  13.2 us (2%)
    psum x1, waiting for transfers between devices, shards(): gram_matrix = lax.psum(partial_gram, ('elem', 'snap'))  247 us
    another operation x14, other arithmetic, shards(): lower_factor = jnp.linalg.cholesky(gram_matrix)  80.6 us
    another operation x3, other arithmetic, shards(): jax.scipy.linalg.solve_triangular(lower_factor, identity_matrix, lower=True)  42.6 us
    gather x4, local copies, waits for them, and re-layouts, shards(): peer_ranks = jnp.take_along_axis(ranks_by_owner, owners, axis=1)  35.9 us
    all_to_all x1, blocking collectives, shards(): lax.all_to_all(projected, 'snap', split_axis=1, concat_axis=2, tiled=True)  29.3 us
    gather x3, local copies, waits for them, and re-layouts, shards(): stored_rows = jnp.where(live_nodes, node_slot[jnp.maximum(node_ids, 0)], 0)  24.1 us
    unnamed x28, local copies, waits for them, and re-layouts  21.4 us
    another operation x12, local copies, waits for them, and re-layouts  13.5 us
  transfers between devices with their start and end apart: 2, of which 1 were waited for; matrix products, arithmetic and copies ran while one was open for 5% of the time, Pallas kernels for 0%

commit v1 on v0

v1 whole, which is shorter than its diff:
```python
import jax
import jax.numpy as jnp
from jax import lax
from jax.experimental import pallas as pl
from jax.experimental.pallas import tpu as pltpu
from jax.sharding import PartitionSpec as P

F32, BF16, I32 = jnp.float32, jnp.bfloat16, jnp.int32
HI = lax.Precision.HIGHEST
MESH = pl.DeviceIdType.MESH
MODES = 512
COLS = 512
ENODES = 8
NDOF = 3
CAP = 16
SAMPLED = 512
N_ELEM = 64
N_SNAP = 4
NODE_DEV = 1024
BAND = MODES // N_SNAP
KROWS = ENODES * NDOF
BLOCKS = [(k, i) for k in range(4) for i in range(k, 4)]


def iota(shape, axis):
    return lax.broadcasted_iota(I32, shape, axis)


def hot(mask):
    return jnp.where(mask, 1.0, 0.0).astype(BF16)


def dot_nt(a, b):
    return lax.dot_general(a, b, (((1,), (1,)), ((), ())), preferred_element_type=F32)


def dot_tn(a, b, precision=None):
    return lax.dot_general(
        a, b, (((0,), (0,)), ((), ())), precision=precision, preferred_element_type=F32
    )


def dot_nn(a, b):
    return jnp.dot(a, b, preferred_element_type=F32)


def index_kernel(
    sample_ref, conn_ref, slot_ref, dev_ref, basis_ref, out_ref, place_ref, basis_v, ids_s, st_s, tab_s, sem
):
    load = pltpu.make_async_copy(basis_ref, basis_v, sem)
    load.start()
    me = lax.axis_index("elem")
    conn = conn_ref[...] + 1
    conn_hi = (conn >> 8).astype(F32)
    conn_lo = (conn & 255).astype(F32)
    conn_t = jnp.concatenate([conn_hi.T, conn_lo.T], 0).astype(BF16)
    sample = sample_ref[...]
    ids = jnp.zeros((16, SAMPLED), F32)
    for part in range(4):
        picks = hot(iota((512, SAMPLED), 0) + 512 * part == sample)
        ids = ids + dot_nn(conn_t[:, 512 * part : 512 * part + 512], picks)
    ids1 = (ids[0:8] * 256.0 + ids[8:16]).astype(I32)
    live = ids1 > 0
    ids_s[...] = jnp.maximum(ids1 - 1, 0)
    table = slot_ref[...]
    tab_s[0:128, :] = (table >> 8).astype(F32).T.astype(BF16)
    tab_s[128:256, :] = (table & 255).astype(F32).T.astype(BF16)

    def lookup(p, carry):
        row = ids_s[pl.ds(p, 1), :]
        picks = hot(iota((512, SAMPLED), 0) == (row >> 7))
        found = dot_nn(tab_s[...], picks)
        here = iota((128, SAMPLED), 0) == (row & 127)
        hi = jnp.sum(jnp.where(here, found[0:128], 0.0), axis=0, keepdims=True)
        lo = jnp.sum(jnp.where(here, found[128:256], 0.0), axis=0, keepdims=True)
        st_s[pl.ds(p, 1), :] = (hi * 256.0 + lo).astype(I32)
        return carry

    lax.fori_loop(0, ENODES, lookup, 0)
    stored = st_s[...]
    owner = stored >> 10
    mine = live & (owner == me)
    has = jnp.max(jnp.where(mine, 1.0, 0.0), axis=0, keepdims=True)
    row = jnp.sum(jnp.where(mine, stored & (NODE_DEV - 1), 0), axis=0, keepdims=True)
    dev = dev_ref[...]
    dev_f = dev.astype(F32)
    dev_col = jnp.broadcast_to(dev_f, (8, SAMPLED)).T[:, 0:1]
    same = hot((dev_col == dev_f) & (iota((SAMPLED, SAMPLED), 0) < iota((SAMPLED, SAMPLED), 1)))
    counts = dot_nn(jnp.where(iota((8, SAMPLED), 0) == 0, has, 1.0).astype(BF16), same)
    rank = counts[0:1].astype(I32)
    slot = counts[1:2].astype(I32)
    q = iota((2 * N_ELEM, SAMPLED), 0)
    goes = hot(((q >> 1) == dev) & ((q & 1) == rank) & (has > 0.5))
    r8 = iota((8, SAMPLED), 0)
    vals = jnp.where(r8 == 0, (row >> 8).astype(F32), jnp.where(r8 == 1, (row & 255).astype(F32), 1.0))
    tab = dot_nt(goes, vals.astype(BF16))
    pick = (tab[:, 0:1] * 256.0 + tab[:, 1:2]).astype(I32)
    valid = tab[:, 2:3] > 0.5
    select = hot((iota((2 * N_ELEM, NODE_DEV), 1) == pick) & valid)
    here = hot((slot == iota((CAP, SAMPLED), 0)) & (dev == me))
    own = dot_nt(here, jnp.where(live, owner + 1, 0).astype(F32).astype(BF16))
    spread = jnp.where((iota((128, CAP), 0) >> 3) == iota((128, CAP), 1), 1.0, 0.0).astype(BF16)
    wide = dot_nn(spread, own.astype(BF16))
    col = jnp.sum(
        jnp.where((iota((128, ENODES), 0) & 7) == iota((128, ENODES), 1), wide, 0.0),
        axis=1,
        keepdims=True,
    )
    by_row = jnp.broadcast_to(col, (128, 128))
    by_col = by_row.T
    before = (iota((128, 128), 1) >> 3) < (iota((128, 128), 0) >> 3)
    ahead = jnp.sum(jnp.where(before & (by_row == by_col), 1.0, 0.0), axis=1, keepdims=True)
    source = ((col - 1.0) * 2.0 + ahead).astype(I32)
    place_ref[...] = hot((iota((128, 128), 1) == source) & (col > 0.5))
    load.wait()
    out_ref[...] = dot_nn(select, basis_v[...]).astype(BF16)


def index_call(sample, conn, slots, dev, basis):
    width = basis.shape[1]
    vm = pl.BlockSpec(memory_space=pltpu.VMEM)
    return pl.pallas_call(
        index_kernel,
        out_shape=(
            jax.ShapeDtypeStruct((2 * N_ELEM, width), BF16),
            jax.ShapeDtypeStruct((128, 128), BF16),
        ),
        in_specs=[vm, vm, vm, vm, pl.BlockSpec(memory_space=pl.ANY)],
        out_specs=(vm, vm),
        scratch_shapes=[
            pltpu.VMEM(basis.shape, BF16),
            pltpu.VMEM((ENODES, SAMPLED), I32),
            pltpu.VMEM((ENODES, SAMPLED), I32),
            pltpu.VMEM((256, 512), BF16),
            pltpu.SemaphoreType.DMA,
        ],
        name="index_tables",
    )(sample, conn, slots, dev, basis)


def split2(x):
    hi = x.astype(BF16)
    return hi, (x - hi.astype(F32)).astype(BF16)


def split3(x):
    h = x.astype(BF16).astype(F32)
    r = x - h
    m = r.astype(BF16).astype(F32)
    return h, m, r - m


def gram_part_kernel(basis_ref, forces_ref, c_ref):
    basis = basis_ref[...]
    forces = forces_ref[...]
    rows = CAP * KROWS
    inner = dot_nt(basis, basis)
    same = (iota((rows, rows), 0) // KROWS) == (iota((rows, rows), 1) // KROWS)
    inner = jnp.where(same, inner, 0.0)
    h, m, l = split3(inner)
    moved = dot_nn(h.astype(BF16), forces) + dot_nn(m.astype(BF16), forces) + dot_nn(l.astype(BF16), forces)
    moved = moved * (1.0 / (SAMPLED * MODES))
    h, m, l = split3(moved)
    h, m, l = h.astype(BF16), m.astype(BF16), l.astype(BF16)
    at = 0
    for k in range(4):
        left = forces[:, 128 * k : 128 * k + 128]
        part = dot_tn(left, h[:, 128 * k :]) + dot_tn(left, m[:, 128 * k :]) + dot_tn(left, l[:, 128 * k :])
        for i in range(4 - k):
            c_ref[at] = part[:, 128 * i : 128 * i + 128].reshape(16, 8, 128)
            at += 1


def gram_part(basis, forces):
    return pl.pallas_call(
        gram_part_kernel,
        out_shape=jax.ShapeDtypeStruct((10, 16, 8, 128), F32),
        name="gram_part",
    )(basis, forces)


def gram_sum_kernel(
    c_ref, o_ref, rbuf, rs_send, rs_recv, own_sem, z_send, z_recv, xy_send, xy_recv, c_send, c_recv
):
    e = lax.axis_index("elem")
    x = lax.axis_index("snap")
    y, z, c = e // 16, (e // 2) % 8, e % 2
    barrier = pltpu.get_barrier_semaphore()

    def greet(j, carry):
        pl.semaphore_signal(barrier, inc=1, device_id=((e + j) % N_ELEM, x), device_id_type=MESH)
        return carry

    lax.fori_loop(1, N_ELEM, greet, 0)

    def greet_x(j, carry):
        x2 = (x + 1 + j // 4) % 4
        y2 = j % 4
        pl.semaphore_signal(
            barrier, inc=1, device_id=(y2 * 16 + z * 2 + c, x2), device_id_type=MESH
        )
        return carry

    lax.fori_loop(0, 12, greet_x, 0)
    pl.semaphore_wait(barrier, N_ELEM - 1 + 12)

    line = y * 2 + c
    k_own = (5 * z + 7) // 8
    owns = (8 * k_own) // 5 == z

    def piece(i):
        t = (i + e) % 40
        ln, k = t // 5, t % 5
        peer = (ln // 2) * 16 + ((8 * k) // 5) * 2 + ln % 2
        copy = pltpu.make_async_remote_copy(
            src_ref=c_ref.at[x * 40 + t],
            dst_ref=rbuf.at[e],
            send_sem=rs_send.at[t],
            recv_sem=rs_recv.at[e],
            device_id=(peer, x),
            device_id_type=MESH,
        )
        return copy, peer

    def scatter(i, carry):
        copy, peer = piece(i)

        @pl.when(peer != e)
        def _():
            copy.start()

        return carry

    lax.fori_loop(0, 40, scatter, 0)
    tile = x * 40 + line * 5 + k_own

    @pl.when(owns)
    def _():
        mine = pltpu.make_async_copy(c_ref.at[tile], rbuf.at[e], own_sem)
        mine.start()
        mine.wait()

        def arrive(j, carry):
            s = (e + j) % N_ELEM
            pltpu.make_async_copy(rbuf.at[s], rbuf.at[s], rs_recv.at[s]).wait()
            return carry

        lax.fori_loop(1, N_ELEM, arrive, 0)
        o_ref[tile] = jnp.sum(rbuf[...], axis=0)
        for dz in range(1, 8):
            z2 = (z + dz) % 8
            pltpu.make_async_remote_copy(
                src_ref=o_ref.at[tile],
                dst_ref=o_ref.at[tile],
                send_sem=z_send.at[dz - 1],
                recv_sem=z_recv.at[k_own],
                device_id=(y * 16 + z2 * 2 + c, x),
                device_id_type=MESH,
            ).start()

    first = x * 40 + line * 5
    for k in range(5):

        @pl.when((8 * k) // 5 != z)
        def _():
            ref = o_ref.at[first + k]
            pltpu.make_async_copy(ref, ref, z_recv.at[k]).wait()

    def chunk_copy(j):
        x2, y2 = (x + j // 4) % 4, (y + j) % 4
        return pltpu.make_async_remote_copy(
            src_ref=o_ref.at[pl.ds(first, 5)],
            dst_ref=o_ref.at[pl.ds(first, 5)],
            send_sem=xy_send.at[j],
            recv_sem=xy_recv.at[x * 4 + y],
            device_id=(y2 * 16 + z * 2 + c, x2),
            device_id_type=MESH,
        )

    def send_chunk(j, carry):
        chunk_copy(j).start()
        return carry

    lax.fori_loop(1, 16, send_chunk, 0)

    def core_copy(j):
        x2, y2 = (x + j // 4) % 4, (y + j) % 4
        n = x2 * 4 + y2
        at = (x2 * 8 + y2 * 2 + c) * 5
        return n, at, pltpu.make_async_remote_copy(
            src_ref=o_ref.at[pl.ds(at, 5)],
            dst_ref=o_ref.at[pl.ds(at, 5)],
            send_sem=c_send.at[n],
            recv_sem=c_recv.at[n],
            device_id=(e + 1 - 2 * c, x),
            device_id_type=MESH,
        )

    core_copy(0)[2].start()

    def forward(j, carry):
        n, at, copy = core_copy(j)
        ref = o_ref.at[pl.ds(at, 5)]
        pltpu.make_async_copy(ref, ref, xy_recv.at[n]).wait()
        copy.start()
        return carry

    lax.fori_loop(1, 16, forward, 0)

    def finish(n, carry):
        other = (n * 2 + 1 - c) * 5
        ref = o_ref.at[pl.ds(other, 5)]
        pltpu.make_async_copy(ref, ref, c_recv.at[n]).wait()
        pltpu.make_async_copy(ref, ref, c_send.at[n]).wait()
        return carry

    lax.fori_loop(0, 16, finish, 0)

    def drain_xy(j, carry):
        ref = o_ref.at[pl.ds(first, 5)]
        pltpu.make_async_copy(ref, ref, xy_send.at[j]).wait()
        return carry

    lax.fori_loop(1, 16, drain_xy, 0)

    @pl.when(owns)
    def _():
        for dz in range(7):
            ref = o_ref.at[tile]
            pltpu.make_async_copy(ref, ref, z_send.at[dz]).wait()

    def drain_rs(i, carry):
        copy, peer = piece(i)

        @pl.when(peer != e)
        def _():
            copy.wait_send()

        return carry

    lax.fori_loop(0, 40, drain_rs, 0)


def gram_sum(parts):
    dma = pltpu.SemaphoreType.DMA
    vm = pl.BlockSpec(memory_space=pltpu.VMEM)
    return pl.pallas_call(
        gram_sum_kernel,
        out_shape=jax.ShapeDtypeStruct((160, 8, 128), F32),
        in_specs=[vm],
        out_specs=vm,
        scratch_shapes=[
            pltpu.VMEM((N_ELEM, 8, 128), F32),
            dma((40,)),
            dma((N_ELEM,)),
            dma,
            dma((7,)),
            dma((5,)),
            dma((16,)),
            dma((16,)),
            dma((16,)),
            dma((16,)),
        ],
        compiler_params=pltpu.CompilerParams(collective_id=1, has_side_effects=True),
        name="gram_sum",
    )(parts)


def panel(p0, p1, lane):
    def rep(v, i):
        return jnp.broadcast_to(v[i : i + 1, :], (8, 128))

    cols = [jnp.broadcast_to(p0[:, lane + j : lane + j + 1], (8, 128)) for j in range(8)]
    a = {(i, j): rep(cols[j], i) for j in range(8) for i in range(j + 1)}
    rows = [[rep(p0, i), rep(p1, i)] for i in range(8)]
    sub = iota((8, 128), 0)
    out = [None, None]
    for k in range(8):
        r = lax.rsqrt(a[k, k])
        u = {j: a[k, j] * r for j in range(k + 1, 8)}
        rows[k] = [v * r for v in rows[k]]
        for i in range(k + 1, 8):
            for j in range(i, 8):
                a[i, j] = a[i, j] - u[i] * u[j]
            rows[i] = [v - u[i] * w for v, w in zip(rows[i], rows[k])]
        for c in range(2):
            out[c] = rows[k][c] if k == 0 else jnp.where(sub == k, rows[k][c], out[c])
    return out


def factor(A, M, W):
    eye = jnp.where(iota((128, 128), 0) == iota((128, 128), 1), 1.0, 0.0)

    def block(k, carry):
        off = pl.multiple_of(k * 128, 128)
        M[:, 0:128] = A[pl.ds(off, 128), pl.ds(off, 128)]
        M[:, 128:256] = eye
        for p in range(16):
            top = 8 * p
            u0, u1 = panel(M[top : top + 8, 0:128], M[top : top + 8, 128:256], top)
            M[top : top + 8, 0:128] = u0
            M[top : top + 8, 128:256] = u1
            if p < 15:
                h0, m0, l0 = split3(u0)
                h1, m1, l1 = split3(u1)
                lhs = jnp.concatenate([h0, h0, m0, m0, h0, l0], 0).astype(BF16)
                r0 = jnp.concatenate([h0, m0, h0, m0, l0, h0], 0)
                r1 = jnp.concatenate([h1, m1, h1, m1, l1, h1], 0)
                upd = dot_tn(lhs, jnp.concatenate([r0, r1], 1).astype(BF16))
                M[top + 8 :, :] = M[top + 8 :, :] - upd[top + 8 :, :]
        inv = M[:, 128:256]
        W[k] = inv
        A[pl.ds(off, 128), :] = jnp.dot(
            inv, A[pl.ds(off, 128), :], precision=HI, preferred_element_type=F32
        )

        def trail(i, carry2):
            o2 = pl.multiple_of(i * 128, 128)
            A[pl.ds(o2, 128), :] = A[pl.ds(o2, 128), :] - dot_tn(
                A[pl.ds(off, 128), pl.ds(o2, 128)], A[pl.ds(off, 128), :], HI
            )
            return carry2

        lax.fori_loop(k + 1, 4, trail, 0)
        return carry

    lax.fori_loop(0, 4, block, 0)


STEP = 2


def finish_kernel(c_ref, f_ref, b_ref, o_ref, t_ref, A, M, W, G):
    @pl.when(pl.program_id(0) == 0)
    def _():
        for n, (k, i) in enumerate(BLOCKS):
            A[128 * k : 128 * k + 128, 128 * i : 128 * i + 128] = c_ref[n].reshape(128, 128)
        factor(A, M, W)
        share = COLS // N_ELEM
        start = pl.multiple_of(lax.axis_index("elem") * share, share)
        upper = A[pl.ds(start, share), :]
        keep = iota((share, COLS), 0) + start <= iota((share, COLS), 1)
        t_ref[...] = jnp.where(keep, upper, 0.0)
        for j in range(4):
            g = f_ref[:, 128 * j : 128 * j + 128].astype(F32)
            for i in range(j):
                g = g - jnp.dot(
                    G[:, 128 * i : 128 * i + 128],
                    A[128 * i : 128 * i + 128, 128 * j : 128 * j + 128],
                    precision=HI,
                    preferred_element_type=F32,
                )
            G[:, 128 * j : 128 * j + 128] = lax.dot_general(
                g, W[j], (((1,), (1,)), ((), ())), precision=HI, preferred_element_type=F32
            )

    for s in range(STEP):
        at = pl.multiple_of((pl.program_id(0) * STEP + s) * KROWS, KROWS)
        h, m, l = split3(G[pl.ds(at, KROWS), :])
        b = b_ref[pl.ds(at, KROWS), :]
        lhs = jnp.concatenate([b, b, b], 0).astype(BF16)
        rhs = jnp.concatenate([h, m, l], 0).astype(BF16)
        o_ref[s] = dot_tn(lhs, rhs)


def finish(gram, forces, band):
    share = COLS // N_ELEM
    whole = lambda shape: pl.BlockSpec(shape, lambda i: (0,) * len(shape))
    return pl.pallas_call(
        finish_kernel,
        grid=(CAP // STEP,),
        out_shape=(
            jax.ShapeDtypeStruct((CAP, BAND, COLS), F32),
            jax.ShapeDtypeStruct((share, COLS), F32),
        ),
        in_specs=[whole((10, 16, 8, 128)), whole((CAP * KROWS, COLS)), whole((CAP * KROWS, BAND))],
        out_specs=(
            pl.BlockSpec((STEP, BAND, COLS), lambda i: (i, 0, 0)),
            whole((share, COLS)),
        ),
        scratch_shapes=[
            pltpu.VMEM((COLS, COLS), F32),
            pltpu.VMEM((128, 256), F32),
            pltpu.VMEM((4, 128, 128), F32),
            pltpu.VMEM((CAP * KROWS, COLS), F32),
        ],
        name="factor_and_apply",
    )(gram, forces, band)


def shards(
    node_basis, stiff_terms, reduced_coords, sample_list, connectivity, node_slot, elem_device
):
    coords = jnp.broadcast_to(reduced_coords[None], (N_SNAP,) + reduced_coords.shape)
    coords = lax.all_to_all(coords, "snap", split_axis=0, concat_axis=0, tiled=True)
    coords = coords.transpose(1, 0, 2).reshape(MODES, -1)
    outgoing, place = index_call(
        sample_list.reshape(1, SAMPLED),
        connectivity,
        node_slot.reshape(512, 128),
        elem_device.reshape(1, SAMPLED),
        node_basis,
    )
    incoming = lax.all_to_all(
        outgoing.reshape(N_ELEM, 2, -1), "elem", split_axis=0, concat_axis=0, tiled=True
    )
    rows = jnp.dot(place, incoming.reshape(2 * N_ELEM, -1), preferred_element_type=F32)
    basis = rows.astype(BF16).reshape(CAP, KROWS, MODES)
    displaced = jnp.einsum(
        "ekm,ms->eks", basis, coords, preferred_element_type=F32
    ).astype(BF16)
    forces = jnp.einsum(
        "tkl,els->ekst", stiff_terms, displaced, preferred_element_type=F32
    ).astype(BF16)
    forces = forces.reshape(CAP * KROWS, COLS)
    basis = basis.reshape(CAP * KROWS, MODES)
    parts = gram_part(basis, forces)
    gram = gram_sum(parts.reshape(160, 8, 128)).reshape(10, 16, 8, 128)
    band = lax.dynamic_slice_in_dim(basis, lax.axis_index("snap") * BAND, BAND, 1)
    return finish(gram, forces, band.astype(F32))


def solution(mesh):
    placed = (P("elem", None), P(), P(None, "snap"), P(), P(), P(), P())
    return jax.shard_map(
        shards,
        mesh=mesh,
        in_specs=placed,
        out_specs=(P("elem", "snap", None), P("elem", None)),
        check_vma=False,
    )
```

time: 639 us -> 131 us (0.21); the launches traced: 630 us -> 131 us
  waiting for transfers between devices: 247 us -> 17.3 us
  other arithmetic: 149 us -> 0.69 us
  local copies, waits for them, and re-layouts: 144 us -> 13.3 us
  Pallas kernels: 0 us -> 78.8 us
  blocking collectives: 29.3 us -> 0 us
  matrix products: 29.9 us -> 3.01 us
  between operations: 17.5 us -> 0.72 us
    psum x1 -> x0, waiting for transfers between devices: 247 us -> none  [shards(): gram_matrix = lax.psum(partial_gram, ('elem', 'snap'))]
    another operation x17 -> x0, other arithmetic: 123 us -> none  [the longest x14 80.6 us: shards(): lower_factor = jnp.linalg.cholesky(gram_matrix)]
    pallas_call x0 -> x4, Pallas kernels: none -> 78.8 us  [the longest x1 35.5 us: finish(): pl.pallas_call(finish_kernel, grid=(CAP // STEP,), out_shape=(jax.ShapeDt...]
    gather x18 -> x0, local copies, waits for them, and re-layouts: 76.6 us -> none  [the longest x4 35.9 us: shards(): peer_ranks = jnp.take_along_axis(ranks_by_owner, owners, axis=1)]
    all_to_all x1 -> x0, blocking collectives: 29.3 us -> none  [shards(): lax.all_to_all(projected, 'snap', split_axis=1, concat_axis=2, tiled=True)]
    unnamed x28 -> x7, local copies, waits for them, and re-layouts: 21.4 us -> 2.2 us
    all_to_all x1 -> x2, waiting for transfers between devices: 0.01 us -> 17.3 us  [the longest x1 14.5 us: shards(): lax.all_to_all(outgoing.reshape(N_ELEM, 2, -1), 'elem', split_axis=0, con...]
    another operation x19 -> x1, local copies, waits for them, and re-layouts: 17.1 us -> 0.19 us  [shards(): basis = basis.reshape(CAP * KROWS, MODES)]
  transfers between devices with their start and end apart: 2 -> 2, of which waited for: 1 -> 2; matrix products, arithmetic and copies ran while one was open for 5% -> 1% of each run, Pallas kernels for 0% -> 0%
where the time goes in v1:
time: 131 us
  Pallas kernels  78.8 us (60%)
  waiting for transfers between devices  17.3 us (13%)
  starting transfers between devices  17.2 us (13%)
  local copies, waits for them, and re-layouts  13.3 us (10%)
  matrix products  3.01 us (2%)
    pallas_call x1, Pallas kernels, finish(): pl.pallas_call(finish_kernel, grid=(CAP // STEP,), out_shape=(jax.ShapeDt...  35.5 us
    pallas_call x1, Pallas kernels, gram_sum(): pl.pallas_call(gram_sum_kernel, out_shape=jax.ShapeDtypeStruct((160, 8, 1...  32.7 us
    all_to_all x1, waiting for transfers between devices, shards(): lax.all_to_all(outgoing.reshape(N_ELEM, 2, -1), 'elem', split_axis=0, con...  14.5 us
    all_to_all x1, starting transfers between devices, shards(): lax.all_to_all(outgoing.reshape(N_ELEM, 2, -1), 'elem', split_axis=0, con...  13.1 us
    pallas_call x1, Pallas kernels, index_call(): pl.pallas_call(index_kernel, out_shape=(jax.ShapeDtypeStruct((2 * N_ELEM,...  6.9 us
    convert_element_type x1, local copies, waits for them, and re-layouts, shards(): forces = jnp.einsum('tkl,els->ekst', stiff_terms, displaced, preferred_el...  4.84 us
    all_to_all x1, starting transfers between devices, shards(): lax.all_to_all(coords, 'snap', split_axis=0, concat_axis=0, tiled=True)  4.02 us
    pallas_call x1, Pallas kernels, gram_part(): pl.pallas_call(gram_part_kernel, out_shape=jax.ShapeDtypeStruct((10, 16,...  3.75 us
  transfers between devices with their start and end apart: 2, of which 2 were waited for; matrix products, arithmetic and copies ran while one was open for 1% of the time, Pallas kernels for 0%

profile of v1, /device:TPU:1, one launch (start us, length us, event | category | flops | bytes accessed | tf_op | source)
XLA Modules:
  0.0 130.9 jit_solution(3116072880992095200)
XLA Ops:
  0.6 0.0 copy-start
  0.6 2.2 %copy.12.conn_ref = s32[2048,8]{1,0:T(8,128)} copy(s32[2048,8]{0,1:T(8,128)} %param.11) | data formatting | bytes 131072 | tf_op args[4]
  2.8 6.9 %index_tables.1 = (bf16[128,1536]{1,0:T(8,128)(2,1)}, bf16[128,128]{1,0:T(8,128)(2,1)}) custom-call(s32[1,512]{1,0:T(1,128)} %bitcast.34, s32[2048,8]{1,0:T(8,128)} %copy.12.conn_ref, s32[512,128]{1,0:T(8,128)} %bitcast.33, s32[1,512]{1,0:T(1,128)} %bitcast.35, bf16[1024,1536]{1,0:T(8,128)(2,1)} %basis_ref.1), custom_call_target="tpu_custom_call" | custom-call | tf_op jit(solution)/shard_map/index_tables/pallas_call | solution.py:122
  9.7 1.9 %reshape.38 = bf16[64,2,1536]{2,1,0:T(2,128)(2,1)} reshape(bf16[128,1536]{1,0:T(8,128)(2,1)} %get-tuple-element.5) | data formatting | bytes 786432 | tf_op jit(solution)/shard_map/reshape | solution.py:505
  11.6 13.1 %all-to-all-start = ((bf16[64,2,1536]{2,1,0:T(2,128)(2,1)}), bf16[64,2,1536]{2,1,0:T(2,128)(2,1)S(1)}, u32[]{:S(2)}, u32[]{:S(2)}) async-start(bf16[64,2,1536]{2,1,0:T(2,128)(2,1)} %reshape.38), calls=%async_computation | async-start | bytes 786432 | tf_op jit(solution)/shard_map/all_to_all | solution.py:504
  24.8 14.5 %all-to-all-done = bf16[64,2,1536]{2,1,0:T(2,128)(2,1)S(1)} async-done(((bf16[64,2,1536]{2,1,0:T(2,128)(2,1)}), bf16[64,2,1536]{2,1,0:T(2,128)(2,1)S(1)}, u32[]{:S(2)}, u32[]{:S(2)}) %all-to-all-start) | async-done | bytes 393248 | tf_op jit(solution)/shard_map/all_to_all | solution.py:504
  39.3 0.0 copy-done.2
  39.3 0.6 broadcast_in_dim.2
  39.9 4.0 %all-to-all-start.1 = ((bf16[4,512,8]{1,2,0:T(8,128)(2,1)}), bf16[4,512,8]{1,2,0:T(8,128)(2,1)S(1)}, u32[]{:S(2)}, u32[]{:S(2)}) async-start(bf16[4,512,8]{1,2,0:T(8,128)(2,1)} %broadcast_in_dim.2), calls=%async_computation.1 | async-start | bytes 65536 | tf_op jit(solution)/shard_map/all_to_all | solution.py:495
  44.0 0.1 reshape.39
  44.1 1.0 convolution_convert_fusion
  45.1 0.2 reshape_reshape.3.basis_ref
  45.3 0.0 copy-start.1
  45.3 0.2 reshape.40
  45.5 2.7 %all-to-all-done.1 = bf16[4,512,8]{1,2,0:T(8,128)(2,1)S(1)} async-done(((bf16[4,512,8]{1,2,0:T(8,128)(2,1)}), bf16[4,512,8]{1,2,0:T(8,128)(2,1)S(1)}, u32[]{:S(2)}, u32[]{:S(2)}) %all-to-all-start.1) | async-done | bytes 32800 | tf_op jit(solution)/shard_map/all_to_all | solution.py:495
  48.3 0.0 copy-done
  48.3 2.0 %fusion = bf16[16,24,32,16]{2,1,3,0:T(8,128)(2,1)} fusion(bf16[16,24,512]{2,1,0:T(8,128)(2,1)S(1)} %reshape.40, bf16[16,24,24]{2,1,0:T(8,128)(2,1)S(1)} %copy-done, bf16[4,512,8]{1,2,0:T(8,128)(2,1)S(1)} %all-to-all-done.1), kind=kOutput, calls=%fused_computation.2 | convolution fusion | flops 22228992 | bytes 837632 | tf_op jit(solution)/shard_map/tkl,els->ekst/dot_general | solution.py:512
  50.3 4.8 %copy.13 = bf16[16,24,32,16]{1,0,3,2:T(8,128)(2,1)S(1)} copy(bf16[16,24,32,16]{2,1,3,0:T(8,128)(2,1)} %fusion) | data formatting | bytes 786432 | tf_op jit(solution)/shard_map/convert_element_type | solution.py:514
  55.1 2.3 %reshape.42 = bf16[384,512]{0,1:T(8,128)(2,1)S(1)} reshape(bf16[16,24,32,16]{1,0,3,2:T(8,128)(2,1)S(1)} %copy.13) | data formatting | bytes 786432 | tf_op jit(solution)/shard_map/reshape | solution.py:515
  57.4 0.9 copy.14.forces_ref.f_ref
  58.4 0.7 dynamic-slice_convert_fusion.b_ref
  59.1 3.7 %gram_part.1 = f32[10,16,8,128]{3,2,1,0:T(8,128)} custom-call(bf16[384,512]{1,0:T(8,128)(2,1)} %copy-done.1, bf16[384,512]{1,0:T(8,128)(2,1)} %copy.14.forces_ref.f_ref), custom_call_target="tpu_custom_call" | custom-call | tf_op jit(solution)/shard_map/gram_part/pallas_call | solution.py:175
  62.8 32.7 %gram_sum.1 = f32[160,8,128]{2,1,0:T(8,128)} custom-call(f32[160,8,128]{2,1,0:T(8,128)} %bitcast.32), custom_call_target="tpu_custom_call" | custom-call | tf_op jit(solution)/shard_map/gram_sum/pallas_call | solution.py:347
  95.5 35.5 %factor_and_apply.1 = (f32[16,128,512]{2,1,0:T(8,128)}, f32[8,512]{1,0:T(8,128)}) custom-call(f32[10,16,8,128]{3,2,1,0:T(8,128)} %bitcast.31, bf16[384,512]{1,0:T(8,128)(2,1)} %copy.14.forces_ref.f_ref, f32[384,128]{1,0:T(8,128)} %dynamic-slice_convert_fusion.b_ref), custom_call_target="tpu_custom_call" | custom-call | tf_op jit(solution)/shard_map/factor_and_apply/pallas_call | solution.py:469
  (2 shorter events, 0.0 us)
Async XLA Ops:
  0.6 47.6 %copy-start = (bf16[16,24,24]{2,1,0:T(8,128)(2,1)S(1)}, bf16[16,24,24]{2,1,0:T(8,128)(2,1)}, u32[]{:S(2)}) copy-start(bf16[16,24,24]{2,1,0:T(8,128)(2,1)} %param.8) | copy-start | bytes 55300
  2.8 36.5 %copy-start.2 = (bf16[512,8]{0,1:T(8,128)(2,1)S(1)}, bf16[512,8]{0,1:T(8,128)(2,1)}, u32[]{:S(2)}) copy-start(bf16[512,8]{0,1:T(8,128)(2,1)} %param.9) | copy-start | bytes 24580
  11.6 27.7 %all-to-all-start = ((bf16[64,2,1536]{2,1,0:T(2,128)(2,1)}), bf16[64,2,1536]{2,1,0:T(2,128)(2,1)S(1)}, u32[]{:S(2)}, u32[]{:S(2)}) async-start(bf16[64,2,1536]{2,1,0:T(2,128)(2,1)} %reshape.38), calls=%async_computation | async-start | bytes 786432 | tf_op jit(solution)/shard_map/all_to_all | solution.py:504
  39.9 8.3 %all-to-all-start.1 = ((bf16[4,512,8]{1,2,0:T(8,128)(2,1)}), bf16[4,512,8]{1,2,0:T(8,128)(2,1)S(1)}, u32[]{:S(2)}, u32[]{:S(2)}) async-start(bf16[4,512,8]{1,2,0:T(8,128)(2,1)} %broadcast_in_dim.2), calls=%async_computation.1 | async-start | bytes 65536 | tf_op jit(solution)/shard_map/all_to_all | solution.py:495
  45.3 13.1 %copy-start.1 = (bf16[384,512]{1,0:T(8,128)(2,1)}, bf16[384,512]{1,0:T(8,128)(2,1)S(1)}, u32[]{:S(2)}) copy-start(bf16[384,512]{1,0:T(8,128)(2,1)S(1)} %reshape_reshape.3.basis_ref) | copy-start | bytes 1179652

commit v2 on v1

--- a/solution.py
+++ b/solution.py
@@ -44,16 +44,17 @@
     return jnp.dot(a, b, preferred_element_type=F32)
 
 
-def index_kernel(
-    sample_ref, conn_ref, slot_ref, dev_ref, basis_ref, out_ref, place_ref, basis_v, ids_s, st_s, tab_s, sem
-):
-    load = pltpu.make_async_copy(basis_ref, basis_v, sem)
-    load.start()
+def split3(x):
+    h = x.astype(BF16).astype(F32)
+    r = x - h
+    m = r.astype(BF16).astype(F32)
+    return h, m, r - m
+
+
+def index_tables(sample_ref, conn_ref, slot_ref, dev_ref, ids_s, st_s, tab_s):
     me = lax.axis_index("elem")
     conn = conn_ref[...] + 1
-    conn_hi = (conn >> 8).astype(F32)
-    conn_lo = (conn & 255).astype(F32)
-    conn_t = jnp.concatenate([conn_hi.T, conn_lo.T], 0).astype(BF16)
+    conn_t = jnp.concatenate([(conn >> 8).astype(F32), (conn & 255).astype(F32)], 0).astype(BF16)
     sample = sample_ref[...]
     ids = jnp.zeros((16, SAMPLED), F32)
     for part in range(4):
@@ -99,7 +100,7 @@
     select = hot((iota((2 * N_ELEM, NODE_DEV), 1) == pick) & valid)
     here = hot((slot == iota((CAP, SAMPLED), 0)) & (dev == me))
     own = dot_nt(here, jnp.where(live, owner + 1, 0).astype(F32).astype(BF16))
-    spread = jnp.where((iota((128, CAP), 0) >> 3) == iota((128, CAP), 1), 1.0, 0.0).astype(BF16)
+    spread = hot((iota((128, CAP), 0) >> 3) == iota((128, CAP), 1))
     wide = dot_nn(spread, own.astype(BF16))
     col = jnp.sum(
         jnp.where((iota((128, ENODES), 0) & 7) == iota((128, ENODES), 1), wide, 0.0),
@@ -111,52 +112,50 @@
     before = (iota((128, 128), 1) >> 3) < (iota((128, 128), 0) >> 3)
     ahead = jnp.sum(jnp.where(before & (by_row == by_col), 1.0, 0.0), axis=1, keepdims=True)
     source = ((col - 1.0) * 2.0 + ahead).astype(I32)
-    place_ref[...] = hot((iota((128, 128), 1) == source) & (col > 0.5))
-    load.wait()
-    out_ref[...] = dot_nn(select, basis_v[...]).astype(BF16)
-
-
-def index_call(sample, conn, slots, dev, basis):
-    width = basis.shape[1]
-    vm = pl.BlockSpec(memory_space=pltpu.VMEM)
-    return pl.pallas_call(
-        index_kernel,
-        out_shape=(
-            jax.ShapeDtypeStruct((2 * N_ELEM, width), BF16),
-            jax.ShapeDtypeStruct((128, 128), BF16),
-        ),
-        in_specs=[vm, vm, vm, vm, pl.BlockSpec(memory_space=pl.ANY)],
-        out_specs=(vm, vm),
-        scratch_shapes=[
-            pltpu.VMEM(basis.shape, BF16),
-            pltpu.VMEM((ENODES, SAMPLED), I32),
-            pltpu.VMEM((ENODES, SAMPLED), I32),
-            pltpu.VMEM((256, 512), BF16),
-            pltpu.SemaphoreType.DMA,
-        ],
-        name="index_tables",
-    )(sample, conn, slots, dev, basis)
-
-
-def split2(x):
-    hi = x.astype(BF16)
-    return hi, (x - hi.astype(F32)).astype(BF16)
-
-
-def split3(x):
-    h = x.astype(BF16).astype(F32)
-    r = x - h
-    m = r.astype(BF16).astype(F32)
-    return h, m, r - m
-
-
-def gram_part_kernel(basis_ref, forces_ref, c_ref):
-    basis = basis_ref[...]
-    forces = forces_ref[...]
-    rows = CAP * KROWS
+    place = hot((iota((128, 128), 1) == source) & (col > 0.5))
+    return select, place
+
+
+def local_forces(place, rows, coords, stiff, b_s, fc_s):
+    n = CAP * KROWS
+    rows = dot_nn(place, rows).astype(BF16)
+    basis = jnp.zeros((n, MODES), F32)
+    for dof in range(NDOF):
+        at = iota((n, 128), 0)
+        rep = hot((at // NDOF == iota((n, 128), 1)) & (at % NDOF == dof))
+        basis = basis + dot_nn(rep, rows[:, MODES * dof : MODES * dof + MODES])
+    basis = basis.astype(BF16)
+    b_s[...] = basis
+    displaced = dot_nt(basis, coords).astype(BF16)
+    every = hot(iota((32, COLS), 1) % 32 == iota((32, COLS), 0))
+    wide = dot_nn(displaced, every)
+    wide = jnp.where(iota((n, COLS), 0) // KROWS == iota((n, COLS), 1) // 32, wide, 0.0).astype(BF16)
+    fold = hot(iota((n, KROWS), 0) % KROWS == iota((n, KROWS), 1))
+    by_elem = dot_tn(fold, wide).astype(BF16)
+    v = dot_nn(stiff, by_elem).astype(BF16).astype(F32)
+    rolled = {}
+    for g in range(4):
+        part = v[:, 128 * g : 128 * g + 128]
+        for shift in range(4):
+            rolled[shift, g] = part if shift == 0 else pltpu.roll(part, 32 * shift, 1)
+    quarter = iota((KROWS, 128), 1) // 32
+    for s in range(CAP):
+        for c in range(4):
+            out = None
+            for b in range(4):
+                t = 4 * c + b
+                piece = rolled[(b - s) % 4, s // 4][KROWS * t : KROWS * t + KROWS, :]
+                out = piece if b == 0 else jnp.where(quarter == b, piece, out)
+            fc_s[KROWS * s : KROWS * s + KROWS, 128 * c : 128 * c + 128] = out
+    i0 = iota((COLS, COLS), 0)
+    order = hot((i0 % 32) * 16 + i0 // 32 == iota((COLS, COLS), 1))
+    return basis, dot_nn(fc_s[...].astype(BF16), order).astype(BF16)
+
+
+def local_gram(basis, forces, c_s):
+    n = CAP * KROWS
     inner = dot_nt(basis, basis)
-    same = (iota((rows, rows), 0) // KROWS) == (iota((rows, rows), 1) // KROWS)
-    inner = jnp.where(same, inner, 0.0)
+    inner = jnp.where(iota((n, n), 0) // KROWS == iota((n, n), 1) // KROWS, inner, 0.0)
     h, m, l = split3(inner)
     moved = dot_nn(h.astype(BF16), forces) + dot_nn(m.astype(BF16), forces) + dot_nn(l.astype(BF16), forces)
     moved = moved * (1.0 / (SAMPLED * MODES))
@@ -167,21 +166,19 @@
         left = forces[:, 128 * k : 128 * k + 128]
         part = dot_tn(left, h[:, 128 * k :]) + dot_tn(left, m[:, 128 * k :]) + dot_tn(left, l[:, 128 * k :])
         for i in range(4 - k):
-            c_ref[at] = part[:, 128 * i : 128 * i + 128].reshape(16, 8, 128)
+            c_s[16 * at : 16 * at + 16] = part[:, 128 * i : 128 * i + 128].reshape(16, 8, 128)
             at += 1
 
 
-def gram_part(basis, forces):
-    return pl.pallas_call(
-        gram_part_kernel,
-        out_shape=jax.ShapeDtypeStruct((10, 16, 8, 128), F32),
-        name="gram_part",
-    )(basis, forces)
-
-
-def gram_sum_kernel(
-    c_ref, o_ref, rbuf, rs_send, rs_recv, own_sem, z_send, z_recv, xy_send, xy_recv, c_send, c_recv
+def panel_kernel(
+    sample_ref, conn_ref, slot_ref, dev_ref, coords_ref, stiff_ref, basis_ref,
+    o_ref, f_ref, band_ref,
+    basis_v, ids_s, st_s, tab_s, out_s, inc_s, ct_s, b_s, fc_s, c_ref, rbuf,
+    load_sem, x_send, x_recv, b_send, b_recv,
+    rs_send, rs_recv, own_sem, z_send, z_recv, xy_send, xy_recv, c_send, c_recv,
 ):
+    load = pltpu.make_async_copy(basis_ref, basis_v, load_sem)
+    load.start()
     e = lax.axis_index("elem")
     x = lax.axis_index("snap")
     y, z, c = e // 16, (e // 2) % 8, e % 2
@@ -202,8 +199,54 @@
         return carry
 
     lax.fori_loop(0, 12, greet_x, 0)
+    select, place = index_tables(sample_ref, conn_ref, slot_ref, dev_ref, ids_s, st_s, tab_s)
+    load.wait()
+    out_s[...] = dot_nn(select, basis_v[...]).astype(BF16).reshape(N_ELEM, 2, NDOF * MODES)
     pl.semaphore_wait(barrier, N_ELEM - 1 + 12)
 
+    def rows_copy(j):
+        peer = (e + j) % N_ELEM
+        return pltpu.make_async_remote_copy(
+            src_ref=out_s.at[peer],
+            dst_ref=inc_s.at[e],
+            send_sem=b_send,
+            recv_sem=b_recv,
+            device_id=(peer, x),
+            device_id_type=MESH,
+        )
+
+    def send_rows(j, carry):
+        rows_copy(j).start()
+        return carry
+
+    lax.fori_loop(1, N_ELEM, send_rows, 0)
+    for j in range(1, N_SNAP):
+        pltpu.make_async_remote_copy(
+            src_ref=coords_ref,
+            dst_ref=ct_s.at[x],
+            send_sem=x_send.at[j - 1],
+            recv_sem=x_recv.at[j - 1],
+            device_id=(e, (x + j) % N_SNAP),
+            device_id_type=MESH,
+        ).start()
+    inc_s[e] = out_s[e]
+    ct_s[x] = coords_ref[...]
+    for j in range(1, N_SNAP):
+        ref = ct_s.at[(x + N_SNAP - j) % N_SNAP]
+        pltpu.make_async_copy(ref, ref, x_recv.at[j - 1]).wait()
+    most = inc_s.at[pl.ds(0, N_ELEM - 1)]
+    pltpu.make_async_copy(most, most, b_recv).wait()
+    basis, forces = local_forces(
+        place,
+        inc_s[...].reshape(2 * N_ELEM, NDOF * MODES),
+        ct_s[...].reshape(32, MODES),
+        stiff_ref[...],
+        b_s,
+        fc_s,
+    )
+    f_ref[...] = forces
+    band_ref[...] = b_s[:, pl.ds(pl.multiple_of(x * BAND, BAND), BAND)]
+    local_gram(basis, forces, c_ref)
     line = y * 2 + c
     k_own = (5 * z + 7) // 8
     owns = (8 * k_own) // 5 == z
@@ -216,7 +259,7 @@
             src_ref=c_ref.at[x * 40 + t],
             dst_ref=rbuf.at[e],
             send_sem=rs_send.at[t],
-            recv_sem=rs_recv.at[e],
+            recv_sem=rs_recv,
             device_id=(peer, x),
             device_id_type=MESH,
         )
@@ -240,12 +283,8 @@
         mine.start()
         mine.wait()
 
-        def arrive(j, carry):
-            s = (e + j) % N_ELEM
-            pltpu.make_async_copy(rbuf.at[s], rbuf.at[s], rs_recv.at[s]).wait()
-            return carry
-
-        lax.fori_loop(1, N_ELEM, arrive, 0)
+        most = rbuf.at[pl.ds(0, N_ELEM - 1)]
+        pltpu.make_async_copy(most, most, rs_recv).wait()
         o_ref[tile] = jnp.sum(rbuf[...], axis=0)
         for dz in range(1, 8):
             z2 = (z + dz) % 8
@@ -341,18 +380,45 @@
     lax.fori_loop(0, 40, drain_rs, 0)
 
 
-def gram_sum(parts):
+    most = inc_s.at[pl.ds(0, N_ELEM - 1)]
+    pltpu.make_async_copy(most, most, b_send).wait()
+    for j in range(1, N_SNAP):
+        pltpu.make_async_copy(coords_ref, coords_ref, x_send.at[j - 1]).wait()
+
+
+def panel_call(sample, conn, slots, dev, coords, stiff, basis):
     dma = pltpu.SemaphoreType.DMA
     vm = pl.BlockSpec(memory_space=pltpu.VMEM)
+    n = CAP * KROWS
+    width = NDOF * MODES
     return pl.pallas_call(
-        gram_sum_kernel,
-        out_shape=jax.ShapeDtypeStruct((160, 8, 128), F32),
-        in_specs=[vm],
-        out_specs=vm,
+        panel_kernel,
+        out_shape=(
+            jax.ShapeDtypeStruct((160, 8, 128), F32),
+            jax.ShapeDtypeStruct((n, COLS), BF16),
+            jax.ShapeDtypeStruct((n, BAND), BF16),
+        ),
+        in_specs=[vm] * 6 + [pl.BlockSpec(memory_space=pl.ANY)],
+        out_specs=(vm, vm, vm),
         scratch_shapes=[
+            pltpu.VMEM((NODE_DEV, width), BF16),
+            pltpu.VMEM((ENODES, SAMPLED), I32),
+            pltpu.VMEM((ENODES, SAMPLED), I32),
+            pltpu.VMEM((256, 512), BF16),
+            pltpu.VMEM((N_ELEM, 2, width), BF16),
+            pltpu.VMEM((N_ELEM, 2, width), BF16),
+            pltpu.VMEM((N_SNAP, 8, MODES), BF16),
+            pltpu.VMEM((n, MODES), BF16),
+            pltpu.VMEM((n, COLS), F32),
+            pltpu.VMEM((160, 8, 128), F32),
             pltpu.VMEM((N_ELEM, 8, 128), F32),
+            dma,
+            dma((3,)),
+            dma((3,)),
+            dma,
+            dma,
             dma((40,)),
-            dma((N_ELEM,)),
+            dma,
             dma,
             dma((7,)),
             dma((5,)),
@@ -362,8 +428,8 @@
             dma((16,)),
         ],
         compiler_params=pltpu.CompilerParams(collective_id=1, has_side_effects=True),
-        name="gram_sum",
-    )(parts)
+        name="panel_exchange",
+    )(sample, conn, slots, dev, coords, stiff, basis)
 
 
 def panel(p0, p1, lane):
@@ -457,7 +523,7 @@
     for s in range(STEP):
         at = pl.multiple_of((pl.program_id(0) * STEP + s) * KROWS, KROWS)
         h, m, l = split3(G[pl.ds(at, KROWS), :])
-        b = b_ref[pl.ds(at, KROWS), :]
+        b = b_ref[pl.ds(at, KROWS), :].astype(F32)
         lhs = jnp.concatenate([b, b, b], 0).astype(BF16)
         rhs = jnp.concatenate([h, m, l], 0).astype(BF16)
         o_ref[s] = dot_tn(lhs, rhs)
@@ -491,33 +557,16 @@
 def shards(
     node_basis, stiff_terms, reduced_coords, sample_list, connectivity, node_slot, elem_device
 ):
-    coords = jnp.broadcast_to(reduced_coords[None], (N_SNAP,) + reduced_coords.shape)
-    coords = lax.all_to_all(coords, "snap", split_axis=0, concat_axis=0, tiled=True)
-    coords = coords.transpose(1, 0, 2).reshape(MODES, -1)
-    outgoing, place = index_call(
+    gram, forces, band = panel_call(
         sample_list.reshape(1, SAMPLED),
-        connectivity,
+        connectivity.T,
         node_slot.reshape(512, 128),
         elem_device.reshape(1, SAMPLED),
+        reduced_coords.T,
+        stiff_terms.reshape(16 * KROWS, KROWS),
         node_basis,
     )
-    incoming = lax.all_to_all(
-        outgoing.reshape(N_ELEM, 2, -1), "elem", split_axis=0, concat_axis=0, tiled=True
-    )
-    rows = jnp.dot(place, incoming.reshape(2 * N_ELEM, -1), preferred_element_type=F32)
-    basis = rows.astype(BF16).reshape(CAP, KROWS, MODES)
-    displaced = jnp.einsum(
-        "ekm,ms->eks", basis, coords, preferred_element_type=F32
-    ).astype(BF16)
-    forces = jnp.einsum(
-        "tkl,els->ekst", stiff_terms, displaced, preferred_element_type=F32
-    ).astype(BF16)
-    forces = forces.reshape(CAP * KROWS, COLS)
-    basis = basis.reshape(CAP * KROWS, MODES)
-    parts = gram_part(basis, forces)
-    gram = gram_sum(parts.reshape(160, 8, 128)).reshape(10, 16, 8, 128)
-    band = lax.dynamic_slice_in_dim(basis, lax.axis_index("snap") * BAND, BAND, 1)
-    return finish(gram, forces, band.astype(F32))
+    return finish(gram.reshape(10, 16, 8, 128), forces, band)
 
 
 def solution(mesh):

time: 131 us -> 90.5 us (0.69)
  waiting for transfers between devices: 17.3 us -> 0 us
  starting transfers between devices: 17.2 us -> 0 us
  local copies, waits for them, and re-layouts: 13.3 us -> 0 us
  Pallas kernels: 78.8 us -> 89.7 us
  matrix products: 3.01 us -> 0 us
    all_to_all x2 -> x0, waiting for transfers between devices: 17.3 us -> none  [the longest x1 14.5 us: shards(): lax.all_to_all(outgoing.reshape(N_ELEM, 2, -1), 'elem', split_axis=0, con...]
    all_to_all x2 -> x0, starting transfers between devices: 17.2 us -> none  [the longest x1 13.1 us: shards(): lax.all_to_all(outgoing.reshape(N_ELEM, 2, -1), 'elem', split_axis=0, con...]
    pallas_call x3 -> x1, Pallas kernels: 43.3 us -> 54.3 us  [panel_call(): pl.pallas_call(panel_kernel, out_shape=(jax.ShapeDtypeStruct((160, 8, 128...]
    reshape x5 -> x0, local copies, waits for them, and re-layouts: 5.48 us -> none  [the longest x2 3.25 us: shards(): forces = forces.reshape(CAP * KROWS, COLS)]
    convert_element_type x1 -> x0, local copies, waits for them, and re-layouts: 4.84 us -> none  [shards(): forces = jnp.einsum('tkl,els->ekst', stiff_terms, displaced, preferred_el...]
    dot_general x2 -> x0, matrix products: 3.01 us -> none  [the longest x1 2.01 us: shards(): jnp.einsum('tkl,els->ekst', stiff_terms, displaced, preferred_element_typ...]
    unnamed x7 -> x0, local copies, waits for them, and re-layouts: 2.2 us -> none
  transfers between devices with their start and end apart: 2 -> 0, of which waited for: 2 -> 0; matrix products, arithmetic and copies ran while one was open for 1% -> 0% of each run, Pallas kernels for 0% -> 0%
where the time goes in v2:
time: 90.5 us; the launch traced here: 90.4 us
  Pallas kernels  89.7 us (99%)
    pallas_call x1, Pallas kernels, panel_call(): pl.pallas_call(panel_kernel, out_shape=(jax.ShapeDtypeStruct((160, 8, 128...  54.3 us
    pallas_call x1, Pallas kernels, finish(): pl.pallas_call(finish_kernel, grid=(CAP // STEP,), out_shape=(jax.ShapeDt...  35.4 us

profile of v2, /device:TPU:1, one launch (start us, length us, event | category | flops | bytes accessed | tf_op | source)
XLA Modules:
  0.0 90.4 jit_solution(6947349260764067963)
XLA Ops:
  0.6 54.3 %panel_exchange.1 = (f32[160,8,128]{2,1,0:T(8,128)}, bf16[384,512]{1,0:T(8,128)(2,1)}, bf16[384,128]{1,0:T(8,128)(2,1)}) custom-call(s32[1,512]{1,0:T(1,128)} %bitcast.12, s32[8,2048]{1,0:T(8,128)} %bitcast.10, s32[512,128]{1,0:T(8,128)} %bitcast.8, s32[1,512]{1,0:T(1,128)} %bitcast.13, bf16[8,512]{1,0:T(8,128)(2,1)} %bitcast.11, bf16[384,24]{1,0:T(8,128)(2,1)} %bitcast.9, ...), custom_call_target="tpu_custom_call" | custom-call | tf_op jit(solution)/shard_map/panel_exchange/pallas_call | solution.py:394
  54.9 35.4 %factor_and_apply.1 = (f32[16,128,512]{2,1,0:T(8,128)}, f32[8,512]{1,0:T(8,128)}) custom-call(f32[10,16,8,128]{3,2,1,0:T(8,128)} %bitcast.7, bf16[384,512]{1,0:T(8,128)(2,1)} %get-tuple-element.6.f_ref, bf16[384,128]{1,0:T(8,128)(2,1)} %get-tuple-element.7.b_ref), custom_call_target="tpu_custom_call" | custom-call | tf_op jit(solution)/shard_map/factor_and_apply/pallas_call | solution.py:535

commit v3 on v2

--- a/solution.py
+++ b/solution.py
@@ -432,38 +432,137 @@
     )(sample, conn, slots, dev, coords, stiff, basis)
 
 
-def panel(p0, p1, lane):
-    def rep(v, i):
-        return jnp.broadcast_to(v[i : i + 1, :], (8, 128))
-
-    cols = [jnp.broadcast_to(p0[:, lane + j : lane + j + 1], (8, 128)) for j in range(8)]
-    a = {(i, j): rep(cols[j], i) for j in range(8) for i in range(j + 1)}
-    rows = [[rep(p0, i), rep(p1, i)] for i in range(8)]
+def split2(x):
+    hi = x.astype(BF16)
+    return hi, (x - hi.astype(F32)).astype(BF16)
+
+
+def rep(v, i):
+    return jnp.broadcast_to(v[i : i + 1, :], (8, 128))
+
+
+def spread_cols(v, lane):
+    return [jnp.broadcast_to(v[:, lane + j : lane + j + 1], (8, 128)) for j in range(8)]
+
+
+def panel(diag, p0, p1, below, ahead):
     sub = iota((8, 128), 0)
     out = [None, None]
     for k in range(8):
-        r = lax.rsqrt(a[k, k])
-        u = {j: a[k, j] * r for j in range(k + 1, 8)}
-        rows[k] = [v * r for v in rows[k]]
-        for i in range(k + 1, 8):
-            for j in range(i, 8):
-                a[i, j] = a[i, j] - u[i] * u[j]
-            rows[i] = [v - u[i] * w for v, w in zip(rows[i], rows[k])]
-        for c in range(2):
-            out[c] = rows[k][c] if k == 0 else jnp.where(sub == k, rows[k][c], out[c])
-    return out
-
-
-def factor(A, M, W):
+        r = lax.rsqrt(rep(diag[k], k))
+        c = diag[k] * r
+        at = {j: rep(c, j) for j in range(k + 1, 8)}
+        for j in range(k + 1, 8):
+            diag[j] = diag[j] - c * at[j]
+        x0, x1 = rep(p0, k) * r, rep(p1, k) * r
+        p0, p1 = p0 - c * x0, p1 - c * x1
+        if k == 0:
+            out = [x0, x1]
+        else:
+            out = [jnp.where(sub == k, x, o) for x, o in zip((x0, x1), out)]
+        if below is not None:
+            c2 = below[k] * r
+            for j in range(k + 1, 8):
+                below[j] = below[j] - c2 * at[j]
+            for j in range(8):
+                ahead[j] = ahead[j] - c2 * rep(c2, j)
+    return out, ahead
+
+
+def product6(a, b):
+    ah, am, al = (v.astype(BF16) for v in split3(a))
+    bh, bm, bl = (v.astype(BF16) for v in split3(b))
+    out = dot_nn(jnp.concatenate([ah, am], 1), jnp.concatenate([bh, bh], 0))
+    out = out + dot_nn(jnp.concatenate([ah, am], 1), jnp.concatenate([bm, bm], 0))
+    return out + dot_nn(jnp.concatenate([ah, al], 1), jnp.concatenate([bl, bh], 0))
+
+
+def product6_tn(a, b):
+    ah, am, al = (v.astype(BF16) for v in split3(a))
+    bh, bm, bl = (v.astype(BF16) for v in split3(b))
+    out = dot_tn(jnp.concatenate([ah, am], 0), jnp.concatenate([bh, bh], 0))
+    out = out + dot_tn(jnp.concatenate([ah, am], 0), jnp.concatenate([bm, bm], 0))
+    return out + dot_tn(jnp.concatenate([ah, al], 0), jnp.concatenate([bl, bh], 0))
+
+
+def finish_kernel(c_ref, f_ref, b_ref, o_ref, t_ref, A, M, uh, um, gf, gh, gm, bf, o_v, sems):
+    for n, (k, i) in enumerate(BLOCKS):
+        A[128 * k : 128 * k + 128, 128 * i : 128 * i + 128] = c_ref[n].reshape(128, 128)
+    for k in range(1, 4):
+        A[128 * k : 128 * k + 128, 0 : 128 * k] = jnp.zeros((128, 128 * k), F32)
+    bf[...] = b_ref[...].astype(F32)
     eye = jnp.where(iota((128, 128), 0) == iota((128, 128), 1), 1.0, 0.0)
-
-    def block(k, carry):
-        off = pl.multiple_of(k * 128, 128)
-        M[:, 0:128] = A[pl.ds(off, 128), pl.ds(off, 128)]
+    upper = iota((128, 128), 0) <= iota((128, 128), 1)
+
+    def across(k, i, inv):
+        def run():
+            rows, cols = slice(128 * k, 128 * k + 128), slice(128 * i, 128 * i + 128)
+            u = product6(inv, A[rows, cols])
+            A[rows, cols] = u
+            uh[rows, cols], um[rows, cols] = split2(u)
+
+        return run
+
+    def trail(k, i, j):
+        def run():
+            done = slice(128 * k, 128 * k + 128)
+            rows, cols = slice(128 * i, 128 * i + 128), slice(128 * j, 128 * j + 128)
+            A[rows, cols] = A[rows, cols] - product6_tn(A[done, rows], A[done, cols])
+
+        return run
+
+    def solve(k, r, inv_h, inv_m):
+        def run():
+            rows = slice(128 * r, 128 * r + 128)
+            cols = slice(128 * k, 128 * k + 128)
+            g = f_ref[rows, cols].astype(F32)
+            if k:
+                done = slice(0, 128 * k)
+                g = g - dot_nn(gh[rows, done], uh[done, cols])
+                g = g - dot_nn(gh[rows, done], um[done, cols])
+                g = g - dot_nn(gm[rows, done], uh[done, cols])
+            h, m = split2(g)
+            g = dot_nt(h, inv_h) + dot_nt(h, inv_m) + dot_nt(m, inv_h)
+            gf[rows, cols] = g
+            h, m = split2(g)
+            gh[rows, cols] = h
+            gm[rows, cols] = m
+
+        return run
+
+    def apply(k, s):
+        def run():
+            rows = slice(KROWS * s, KROWS * s + KROWS)
+            cols = slice(128 * k, 128 * k + 128)
+            g = gf[rows, cols]
+            h = g.astype(BF16).astype(F32)
+            b = bf[rows, :]
+            lhs = jnp.concatenate([b, b], 0).astype(BF16)
+            rhs = jnp.concatenate([h, g - h], 0).astype(BF16)
+            o_v[s, :, cols] = dot_tn(lhs, rhs)
+
+        return run
+
+    def store(k):
+        cols = pl.ds(128 * k, 128)
+        return pltpu.make_async_copy(o_v.at[:, :, cols], o_ref.at[:, :, cols], sems.at[k])
+
+    fill = []
+    for k in range(4):
+        lo = 128 * k
+        M[:, 0:128] = A[lo : lo + 128, lo : lo + 128]
         M[:, 128:256] = eye
+        per = -(-len(fill) // 16)
+        diag = spread_cols(M[0:8, 0:128], 0)
         for p in range(16):
             top = 8 * p
-            u0, u1 = panel(M[top : top + 8, 0:128], M[top : top + 8, 128:256], top)
+            below = ahead = None
+            if p < 15:
+                under = M[top + 8 : top + 16, 0:128]
+                below, ahead = spread_cols(under, top), spread_cols(under, top + 8)
+            (u0, u1), diag = panel(
+                diag, M[top : top + 8, 0:128], M[top : top + 8, 128:256], below, ahead
+            )
             M[top : top + 8, 0:128] = u0
             M[top : top + 8, 128:256] = u1
             if p < 15:
@@ -473,82 +572,57 @@
                 r0 = jnp.concatenate([h0, m0, h0, m0, l0, h0], 0)
                 r1 = jnp.concatenate([h1, m1, h1, m1, l1, h1], 0)
                 upd = dot_tn(lhs, jnp.concatenate([r0, r1], 1).astype(BF16))
-                M[top + 8 :, :] = M[top + 8 :, :] - upd[top + 8 :, :]
+                if p < 12:
+                    M[top + 8 :, :] = M[top + 8 :, :] - upd[top + 8 :, :]
+                else:
+                    later = iota((32, 256), 0) + 96 >= top + 8
+                    M[96:, :] = M[96:, :] - jnp.where(later, upd[96:, :], 0.0)
+            for job in fill[per * p : per * p + per]:
+                job()
         inv = M[:, 128:256]
-        W[k] = inv
-        A[pl.ds(off, 128), :] = jnp.dot(
-            inv, A[pl.ds(off, 128), :], precision=HI, preferred_element_type=F32
-        )
-
-        def trail(i, carry2):
-            o2 = pl.multiple_of(i * 128, 128)
-            A[pl.ds(o2, 128), :] = A[pl.ds(o2, 128), :] - dot_tn(
-                A[pl.ds(off, 128), pl.ds(o2, 128)], A[pl.ds(off, 128), :], HI
-            )
-            return carry2
-
-        lax.fori_loop(k + 1, 4, trail, 0)
-        return carry
-
-    lax.fori_loop(0, 4, block, 0)
-
-
-STEP = 2
-
-
-def finish_kernel(c_ref, f_ref, b_ref, o_ref, t_ref, A, M, W, G):
-    @pl.when(pl.program_id(0) == 0)
-    def _():
-        for n, (k, i) in enumerate(BLOCKS):
-            A[128 * k : 128 * k + 128, 128 * i : 128 * i + 128] = c_ref[n].reshape(128, 128)
-        factor(A, M, W)
-        share = COLS // N_ELEM
-        start = pl.multiple_of(lax.axis_index("elem") * share, share)
-        upper = A[pl.ds(start, share), :]
-        keep = iota((share, COLS), 0) + start <= iota((share, COLS), 1)
-        t_ref[...] = jnp.where(keep, upper, 0.0)
-        for j in range(4):
-            g = f_ref[:, 128 * j : 128 * j + 128].astype(F32)
-            for i in range(j):
-                g = g - jnp.dot(
-                    G[:, 128 * i : 128 * i + 128],
-                    A[128 * i : 128 * i + 128, 128 * j : 128 * j + 128],
-                    precision=HI,
-                    preferred_element_type=F32,
-                )
-            G[:, 128 * j : 128 * j + 128] = lax.dot_general(
-                g, W[j], (((1,), (1,)), ((), ())), precision=HI, preferred_element_type=F32
-            )
-
-    for s in range(STEP):
-        at = pl.multiple_of((pl.program_id(0) * STEP + s) * KROWS, KROWS)
-        h, m, l = split3(G[pl.ds(at, KROWS), :])
-        b = b_ref[pl.ds(at, KROWS), :].astype(F32)
-        lhs = jnp.concatenate([b, b, b], 0).astype(BF16)
-        rhs = jnp.concatenate([h, m, l], 0).astype(BF16)
-        o_ref[s] = dot_tn(lhs, rhs)
+        A[lo : lo + 128, lo : lo + 128] = jnp.where(upper, M[:, 0:128], 0.0)
+        inv_h, inv_m = split2(inv)
+        fill = []
+        if k < 3:
+            across(k, k + 1, inv)()
+            trail(k, k + 1, k + 1)()
+            fill += [across(k, i, inv) for i in range(k + 2, 4)]
+            fill += [trail(k, i, j) for i in range(k + 1, 4) for j in range(i, 4) if j > k + 1]
+        fill += [solve(k, r, inv_h, inv_m) for r in range(3)]
+        fill += [apply(k, s) for s in range(CAP)]
+        fill.append(store(k).start)
+    for job in fill:
+        job()
+    share = COLS // N_ELEM
+    start = pl.multiple_of(lax.axis_index("elem") * share, share)
+    t_ref[...] = A[pl.ds(start, share), :]
+    for k in range(4):
+        store(k).wait()
 
 
 def finish(gram, forces, band):
     share = COLS // N_ELEM
-    whole = lambda shape: pl.BlockSpec(shape, lambda i: (0,) * len(shape))
+    rows = CAP * KROWS
+    vm = pl.BlockSpec(memory_space=pltpu.VMEM)
     return pl.pallas_call(
         finish_kernel,
-        grid=(CAP // STEP,),
         out_shape=(
             jax.ShapeDtypeStruct((CAP, BAND, COLS), F32),
             jax.ShapeDtypeStruct((share, COLS), F32),
         ),
-        in_specs=[whole((10, 16, 8, 128)), whole((CAP * KROWS, COLS)), whole((CAP * KROWS, BAND))],
-        out_specs=(
-            pl.BlockSpec((STEP, BAND, COLS), lambda i: (i, 0, 0)),
-            whole((share, COLS)),
-        ),
+        in_specs=[vm, vm, vm],
+        out_specs=(pl.BlockSpec(memory_space=pl.ANY), vm),
         scratch_shapes=[
             pltpu.VMEM((COLS, COLS), F32),
             pltpu.VMEM((128, 256), F32),
-            pltpu.VMEM((4, 128, 128), F32),
-            pltpu.VMEM((CAP * KROWS, COLS), F32),
+            pltpu.VMEM((COLS, COLS), BF16),
+            pltpu.VMEM((COLS, COLS), BF16),
+            pltpu.VMEM((rows, COLS), F32),
+            pltpu.VMEM((rows, COLS), BF16),
+            pltpu.VMEM((rows, COLS), BF16),
+            pltpu.VMEM((rows, BAND), F32),
+            pltpu.VMEM((CAP, BAND, COLS), F32),
+            pltpu.SemaphoreType.DMA((4,)),
         ],
         name="factor_and_apply",
     )(gram, forces, band)

time: 90.5 us -> 74.6 us (0.82)
  Pallas kernels: 89.7 us -> 73.7 us
    pallas_call x1, Pallas kernels: 35.4 us -> 19.4 us  [finish(): pl.pallas_call(finish_kernel, out_shape=(jax.ShapeDtypeStruct((CAP, BAND,...]
where the time goes in v3:
time: 74.6 us; the launch traced here: 74.5 us
  Pallas kernels  73.7 us (99%)
  between operations  0.8 us (1%)
    pallas_call x1, Pallas kernels, panel_call(): pl.pallas_call(panel_kernel, out_shape=(jax.ShapeDtypeStruct((160, 8, 128...  54.3 us
    pallas_call x1, Pallas kernels, finish(): pl.pallas_call(finish_kernel, out_shape=(jax.ShapeDtypeStruct((CAP, BAND,...  19.4 us

profile of v3, /device:TPU:1, one launch (start us, length us, event | category | flops | bytes accessed | tf_op | source)
XLA Modules:
  0.0 74.5 jit_solution(6601750286042956865)
XLA Ops:
  0.6 54.3 %panel_exchange.1 = (f32[160,8,128]{2,1,0:T(8,128)}, bf16[384,512]{1,0:T(8,128)(2,1)}, bf16[384,128]{1,0:T(8,128)(2,1)}) custom-call(s32[1,512]{1,0:T(1,128)} %bitcast.12, s32[8,2048]{1,0:T(8,128)} %bitcast.10, s32[512,128]{1,0:T(8,128)} %bitcast.8, s32[1,512]{1,0:T(1,128)} %bitcast.13, bf16[8,512]{1,0:T(8,128)(2,1)} %bitcast.11, bf16[384,24]{1,0:T(8,128)(2,1)} %bitcast.9, ...), custom_call_target="tpu_custom_call" | custom-call | tf_op jit(solution)/shard_map/panel_exchange/pallas_call | solution.py:394
  54.9 19.4 %factor_and_apply.1 = (f32[16,128,512]{2,1,0:T(8,128)}, f32[8,512]{1,0:T(8,128)}) custom-call(f32[10,16,8,128]{3,2,1,0:T(8,128)} %bitcast.7, bf16[384,512]{1,0:T(8,128)(2,1)} %get-tuple-element.6.f_ref, bf16[384,128]{1,0:T(8,128)(2,1)} %get-tuple-element.7.b_ref), custom_call_target="tpu_custom_call" | custom-call | tf_op jit(solution)/shard_map/factor_and_apply/pallas_call | solution.py:607

commit v4 on v3

--- a/solution.py
+++ b/solution.py
@@ -67,17 +67,17 @@
     tab_s[0:128, :] = (table >> 8).astype(F32).T.astype(BF16)
     tab_s[128:256, :] = (table & 255).astype(F32).T.astype(BF16)
 
-    def lookup(p, carry):
-        row = ids_s[pl.ds(p, 1), :]
+    def lookup(p):
+        row = ids_s[p : p + 1, :]
         picks = hot(iota((512, SAMPLED), 0) == (row >> 7))
         found = dot_nn(tab_s[...], picks)
         here = iota((128, SAMPLED), 0) == (row & 127)
         hi = jnp.sum(jnp.where(here, found[0:128], 0.0), axis=0, keepdims=True)
         lo = jnp.sum(jnp.where(here, found[128:256], 0.0), axis=0, keepdims=True)
-        st_s[pl.ds(p, 1), :] = (hi * 256.0 + lo).astype(I32)
-        return carry
-
-    lax.fori_loop(0, ENODES, lookup, 0)
+        st_s[p : p + 1, :] = (hi * 256.0 + lo).astype(I32)
+
+    for p in range(ENODES):
+        lookup(p)
     stored = st_s[...]
     owner = stored >> 10
     mine = live & (owner == me)
@@ -172,27 +172,28 @@
 
 def panel_kernel(
     sample_ref, conn_ref, slot_ref, dev_ref, coords_ref, stiff_ref, basis_ref,
-    o_ref, f_ref, band_ref,
-    basis_v, ids_s, st_s, tab_s, out_s, inc_s, ct_s, b_s, fc_s, c_ref, rbuf,
+    gram_ref, f_ref, band_ref,
+    basis_v, ids_s, st_s, tab_s, out_s, inc_s, ct_s, b_s, fc_s, c_ref, rbuf, o_ref, f_v, band_v,
     load_sem, x_send, x_recv, b_send, b_recv,
     rs_send, rs_recv, own_sem, z_send, z_recv, xy_send, xy_recv, c_send, c_recv,
+    gram_sem, f_sem, band_sem,
 ):
     load = pltpu.make_async_copy(basis_ref, basis_v, load_sem)
     load.start()
     e = lax.axis_index("elem")
     x = lax.axis_index("snap")
-    y, z, c = e // 16, (e // 2) % 8, e % 2
+    y, z, c = e >> 4, (e >> 1) & 7, e & 1
     barrier = pltpu.get_barrier_semaphore()
 
     def greet(j, carry):
-        pl.semaphore_signal(barrier, inc=1, device_id=((e + j) % N_ELEM, x), device_id_type=MESH)
+        pl.semaphore_signal(barrier, inc=1, device_id=((e + j) & (N_ELEM - 1), x), device_id_type=MESH)
         return carry
 
     lax.fori_loop(1, N_ELEM, greet, 0)
 
     def greet_x(j, carry):
-        x2 = (x + 1 + j // 4) % 4
-        y2 = j % 4
+        x2 = (x + 1 + (j >> 2)) & 3
+        y2 = j & 3
         pl.semaphore_signal(
             barrier, inc=1, device_id=(y2 * 16 + z * 2 + c, x2), device_id_type=MESH
         )
@@ -205,7 +206,7 @@
     pl.semaphore_wait(barrier, N_ELEM - 1 + 12)
 
     def rows_copy(j):
-        peer = (e + j) % N_ELEM
+        peer = (e + j) & (N_ELEM - 1)
         return pltpu.make_async_remote_copy(
             src_ref=out_s.at[peer],
             dst_ref=inc_s.at[e],
@@ -244,88 +245,88 @@
         b_s,
         fc_s,
     )
-    f_ref[...] = forces
-    band_ref[...] = b_s[:, pl.ds(pl.multiple_of(x * BAND, BAND), BAND)]
+    f_v[...] = forces
+    band_v[...] = b_s[:, pl.ds(pl.multiple_of(x * BAND, BAND), BAND)]
+    f_out = pltpu.make_async_copy(f_v, f_ref, f_sem)
+    band_out = pltpu.make_async_copy(band_v, band_ref, band_sem)
     local_gram(basis, forces, c_ref)
     line = y * 2 + c
-    k_own = (5 * z + 7) // 8
-    owns = (8 * k_own) // 5 == z
-
-    def piece(i):
-        t = (i + e) % 40
-        ln, k = t // 5, t % 5
-        peer = (ln // 2) * 16 + ((8 * k) // 5) * 2 + ln % 2
-        copy = pltpu.make_async_remote_copy(
-            src_ref=c_ref.at[x * 40 + t],
-            dst_ref=rbuf.at[e],
-            send_sem=rs_send.at[t],
-            recv_sem=rs_recv,
-            device_id=(peer, x),
-            device_id_type=MESH,
-        )
-        return copy, peer
+    k_own = (5 * z + 7) >> 3
+    owns = ((k_own * 104) >> 6) == z
 
     def scatter(i, carry):
-        copy, peer = piece(i)
+        v = i + e
+        t = v - 40 * ((v * 205) >> 13)
+        ln = (t * 205) >> 10
+        k = t - 5 * ln
+        peer = ((ln >> 1) << 4) + (((k * 104) >> 6) << 1) + (ln & 1)
 
         @pl.when(peer != e)
         def _():
-            copy.start()
+            pltpu.make_async_remote_copy(
+                src_ref=c_ref.at[x * 40 + t],
+                dst_ref=rbuf.at[e],
+                send_sem=rs_send,
+                recv_sem=rs_recv,
+                device_id=(peer, x),
+                device_id_type=MESH,
+            ).start()
 
         return carry
 
     lax.fori_loop(0, 40, scatter, 0)
-    tile = x * 40 + line * 5 + k_own
+    f_out.start()
+    band_out.start()
+    first = x * 40 + line * 5
+    tile = first + k_own
 
     @pl.when(owns)
     def _():
         mine = pltpu.make_async_copy(c_ref.at[tile], rbuf.at[e], own_sem)
         mine.start()
         mine.wait()
-
         most = rbuf.at[pl.ds(0, N_ELEM - 1)]
         pltpu.make_async_copy(most, most, rs_recv).wait()
         o_ref[tile] = jnp.sum(rbuf[...], axis=0)
-        for dz in range(1, 8):
-            z2 = (z + dz) % 8
+        for dz in (1, 7, 2, 6, 3, 5, 4):
+            z2 = (z + dz) & 7
             pltpu.make_async_remote_copy(
                 src_ref=o_ref.at[tile],
                 dst_ref=o_ref.at[tile],
                 send_sem=z_send.at[dz - 1],
                 recv_sem=z_recv.at[k_own],
-                device_id=(y * 16 + z2 * 2 + c, x),
+                device_id=((y << 4) + (z2 << 1) + c, x),
                 device_id_type=MESH,
             ).start()
 
-    first = x * 40 + line * 5
-    for k in range(5):
-
-        @pl.when((8 * k) // 5 != z)
+    near = k_own - 5 * ((k_own * 205) >> 10)
+    for step in (0, 1, 4, 2, 3):
+        v = near + step
+        k = v - 5 * ((v * 205) >> 10)
+        at = first + k
+
+        @pl.when(((k * 104) >> 6) != z)
         def _():
-            ref = o_ref.at[first + k]
-            pltpu.make_async_copy(ref, ref, z_recv.at[k]).wait()
-
-    def chunk_copy(j):
-        x2, y2 = (x + j // 4) % 4, (y + j) % 4
-        return pltpu.make_async_remote_copy(
-            src_ref=o_ref.at[pl.ds(first, 5)],
-            dst_ref=o_ref.at[pl.ds(first, 5)],
-            send_sem=xy_send.at[j],
-            recv_sem=xy_recv.at[x * 4 + y],
-            device_id=(y2 * 16 + z * 2 + c, x2),
-            device_id_type=MESH,
-        )
-
-    def send_chunk(j, carry):
-        chunk_copy(j).start()
-        return carry
-
-    lax.fori_loop(1, 16, send_chunk, 0)
+            pltpu.make_async_copy(o_ref.at[at], o_ref.at[at], z_recv.at[k]).wait()
+
+        def send_tile(j, carry):
+            x2, y2 = (x + (j >> 2)) & 3, (y + j) & 3
+            pltpu.make_async_remote_copy(
+                src_ref=o_ref.at[at],
+                dst_ref=o_ref.at[at],
+                send_sem=xy_send,
+                recv_sem=xy_recv.at[x * 4 + y],
+                device_id=((y2 << 4) + (z << 1) + c, x2),
+                device_id_type=MESH,
+            ).start()
+            return carry
+
+        lax.fori_loop(1, 16, send_tile, 0)
 
     def core_copy(j):
-        x2, y2 = (x + j // 4) % 4, (y + j) % 4
+        x2, y2 = (x + (j >> 2)) & 3, (y + j) & 3
         n = x2 * 4 + y2
-        at = (x2 * 8 + y2 * 2 + c) * 5
+        at = (n * 2 + c) * 5
         return n, at, pltpu.make_async_remote_copy(
             src_ref=o_ref.at[pl.ds(at, 5)],
             dst_ref=o_ref.at[pl.ds(at, 5)],
@@ -335,51 +336,50 @@
             device_id_type=MESH,
         )
 
+    def put(at):
+        pltpu.make_async_copy(o_ref.at[pl.ds(at, 5)], gram_ref.at[pl.ds(at, 5)], gram_sem).start()
+
     core_copy(0)[2].start()
+    put(first)
 
     def forward(j, carry):
         n, at, copy = core_copy(j)
         ref = o_ref.at[pl.ds(at, 5)]
         pltpu.make_async_copy(ref, ref, xy_recv.at[n]).wait()
         copy.start()
+        put(at)
         return carry
 
     lax.fori_loop(1, 16, forward, 0)
 
-    def finish(n, carry):
+    def finish_core(n, carry):
         other = (n * 2 + 1 - c) * 5
         ref = o_ref.at[pl.ds(other, 5)]
         pltpu.make_async_copy(ref, ref, c_recv.at[n]).wait()
+        put(other)
         pltpu.make_async_copy(ref, ref, c_send.at[n]).wait()
         return carry
 
-    lax.fori_loop(0, 16, finish, 0)
-
-    def drain_xy(j, carry):
-        ref = o_ref.at[pl.ds(first, 5)]
-        pltpu.make_async_copy(ref, ref, xy_send.at[j]).wait()
-        return carry
-
-    lax.fori_loop(1, 16, drain_xy, 0)
+    lax.fori_loop(0, 16, finish_core, 0)
+    sent = o_ref.at[pl.ds(0, 75)]
+    pltpu.make_async_copy(sent, sent, xy_send).wait()
 
     @pl.when(owns)
     def _():
         for dz in range(7):
             ref = o_ref.at[tile]
             pltpu.make_async_copy(ref, ref, z_send.at[dz]).wait()
-
-    def drain_rs(i, carry):
-        copy, peer = piece(i)
-
-        @pl.when(peer != e)
-        def _():
-            copy.wait_send()
-
-        return carry
-
-    lax.fori_loop(0, 40, drain_rs, 0)
-
-
+        ref = c_ref.at[pl.ds(0, 39)]
+        pltpu.make_async_copy(ref, ref, rs_send).wait()
+
+    @pl.when(jnp.logical_not(owns))
+    def _():
+        ref = c_ref.at[pl.ds(0, 40)]
+        pltpu.make_async_copy(ref, ref, rs_send).wait()
+
+    f_out.wait()
+    band_out.wait()
+    pltpu.make_async_copy(o_ref, gram_ref, gram_sem).wait()
     most = inc_s.at[pl.ds(0, N_ELEM - 1)]
     pltpu.make_async_copy(most, most, b_send).wait()
     for j in range(1, N_SNAP):
@@ -399,7 +399,7 @@
             jax.ShapeDtypeStruct((n, BAND), BF16),
         ),
         in_specs=[vm] * 6 + [pl.BlockSpec(memory_space=pl.ANY)],
-        out_specs=(vm, vm, vm),
+        out_specs=(pl.BlockSpec(memory_space=pl.ANY),) * 3,
         scratch_shapes=[
             pltpu.VMEM((NODE_DEV, width), BF16),
             pltpu.VMEM((ENODES, SAMPLED), I32),
@@ -412,20 +412,26 @@
             pltpu.VMEM((n, COLS), F32),
             pltpu.VMEM((160, 8, 128), F32),
             pltpu.VMEM((N_ELEM, 8, 128), F32),
+            pltpu.VMEM((160, 8, 128), F32),
+            pltpu.VMEM((n, COLS), BF16),
+            pltpu.VMEM((n, BAND), BF16),
             dma,
             dma((3,)),
             dma((3,)),
             dma,
             dma,
-            dma((40,)),
+            dma,
             dma,
             dma,
             dma((7,)),
             dma((5,)),
+            dma,
             dma((16,)),
             dma((16,)),
             dma((16,)),
-            dma((16,)),
+            dma,
+            dma,
+            dma,
         ],
         compiler_params=pltpu.CompilerParams(collective_id=1, has_side_effects=True),
         name="panel_exchange",
@@ -485,12 +491,20 @@
     return out + dot_tn(jnp.concatenate([ah, al], 0), jnp.concatenate([bl, bh], 0))
 
 
-def finish_kernel(c_ref, f_ref, b_ref, o_ref, t_ref, A, M, uh, um, gf, gh, gm, bf, o_v, sems):
+def finish_kernel(
+    c_hbm, f_hbm, b_hbm, o_ref, t_ref, A, M, uh, um, gf, gh, gm, bf, o_v, c_ref, f_ref, b_ref, sems, loads
+):
+    get_c = pltpu.make_async_copy(c_hbm, c_ref, loads.at[0])
+    get_f = pltpu.make_async_copy(f_hbm, f_ref, loads.at[1])
+    get_b = pltpu.make_async_copy(b_hbm, b_ref, loads.at[2])
+    get_c.start()
+    get_f.start()
+    get_b.start()
+    get_c.wait()
     for n, (k, i) in enumerate(BLOCKS):
         A[128 * k : 128 * k + 128, 128 * i : 128 * i + 128] = c_ref[n].reshape(128, 128)
     for k in range(1, 4):
         A[128 * k : 128 * k + 128, 0 : 128 * k] = jnp.zeros((128, 128 * k), F32)
-    bf[...] = b_ref[...].astype(F32)
     eye = jnp.where(iota((128, 128), 0) == iota((128, 128), 1), 1.0, 0.0)
     upper = iota((128, 128), 0) <= iota((128, 128), 1)
 
@@ -583,6 +597,10 @@
         A[lo : lo + 128, lo : lo + 128] = jnp.where(upper, M[:, 0:128], 0.0)
         inv_h, inv_m = split2(inv)
         fill = []
+        if k == 0:
+            get_f.wait()
+            get_b.wait()
+            bf[...] = b_ref[...].astype(F32)
         if k < 3:
             across(k, k + 1, inv)()
             trail(k, k + 1, k + 1)()
@@ -610,7 +628,7 @@
             jax.ShapeDtypeStruct((CAP, BAND, COLS), F32),
             jax.ShapeDtypeStruct((share, COLS), F32),
         ),
-        in_specs=[vm, vm, vm],
+        in_specs=[pl.BlockSpec(memory_space=pl.ANY)] * 3,
         out_specs=(pl.BlockSpec(memory_space=pl.ANY), vm),
         scratch_shapes=[
             pltpu.VMEM((COLS, COLS), F32),
@@ -622,7 +640,11 @@
             pltpu.VMEM((rows, COLS), BF16),
             pltpu.VMEM((rows, BAND), F32),
             pltpu.VMEM((CAP, BAND, COLS), F32),
+            pltpu.VMEM((10, 16, 8, 128), F32),
+            pltpu.VMEM((rows, COLS), BF16),
+            pltpu.VMEM((rows, BAND), BF16),
             pltpu.SemaphoreType.DMA((4,)),
+            pltpu.SemaphoreType.DMA((3,)),
         ],
         name="factor_and_apply",
     )(gram, forces, band)

time: 74.6 us -> 70.2 us (0.941)
  Pallas kernels: 73.7 us -> 69.2 us
    pallas_call x1, Pallas kernels: 54.3 us -> 49.8 us  [panel_call(): pl.pallas_call(panel_kernel, out_shape=(jax.ShapeDtypeStruct((160, 8, 128...]
where the time goes in v4:
time: 70.2 us; the launch traced here: 70 us
  Pallas kernels  69.2 us (99%)
  between operations  0.8 us (1%)
    pallas_call x1, Pallas kernels, panel_call(): pl.pallas_call(panel_kernel, out_shape=(jax.ShapeDtypeStruct((160, 8, 128...  49.8 us
    pallas_call x1, Pallas kernels, finish(): pl.pallas_call(finish_kernel, out_shape=(jax.ShapeDtypeStruct((CAP, BAND,...  19.4 us

profile of v4, /device:TPU:1, one launch (start us, length us, event | category | flops | bytes accessed | tf_op | source)
XLA Modules:
  0.0 70.0 jit_solution(6037752257966644238)
XLA Ops:
  0.6 49.8 %panel_exchange.1 = (f32[160,8,128]{2,1,0:T(8,128)}, bf16[384,512]{1,0:T(8,128)(2,1)}, bf16[384,128]{1,0:T(8,128)(2,1)}) custom-call(s32[1,512]{1,0:T(1,128)} %bitcast.12, s32[8,2048]{1,0:T(8,128)} %bitcast.10, s32[512,128]{1,0:T(8,128)} %bitcast.8, s32[1,512]{1,0:T(1,128)} %bitcast.13, bf16[8,512]{1,0:T(8,128)(2,1)} %bitcast.11, bf16[384,24]{1,0:T(8,128)(2,1)} %bitcast.9, ...), custom_call_target="tpu_custom_call" | custom-call | tf_op jit(solution)/shard_map/panel_exchange/pallas_call | solution.py:394
  50.4 19.4 %factor_and_apply.1 = (f32[16,128,512]{2,1,0:T(8,128)}, f32[8,512]{1,0:T(8,128)}) custom-call(f32[10,16,8,128]{3,2,1,0:T(8,128)} %bitcast.7, bf16[384,512]{1,0:T(8,128)(2,1)} %get-tuple-element.6.f_hbm, bf16[384,128]{1,0:T(8,128)(2,1)} %get-tuple-element.7.b_hbm), custom_call_target="tpu_custom_call" | custom-call | tf_op jit(solution)/shard_map/factor_and_apply/pallas_call | solution.py:625

commit v5 on v4

--- a/solution.py
+++ b/solution.py
@@ -54,12 +54,14 @@
 def index_tables(sample_ref, conn_ref, slot_ref, dev_ref, ids_s, st_s, tab_s):
     me = lax.axis_index("elem")
     conn = conn_ref[...] + 1
-    conn_t = jnp.concatenate([(conn >> 8).astype(F32), (conn & 255).astype(F32)], 0).astype(BF16)
+    conn_t = jnp.concatenate([(conn >> 8).astype(F32), (conn & 255).astype(F32)], 0)
     sample = sample_ref[...]
+    groups = 2048 // 128
+    stacked = jnp.concatenate([conn_t[:, 128 * g : 128 * g + 128] for g in range(groups)], 0)
+    found = dot_nn(stacked.astype(BF16), hot(iota((128, SAMPLED), 0) == (sample & 127)))
     ids = jnp.zeros((16, SAMPLED), F32)
-    for part in range(4):
-        picks = hot(iota((512, SAMPLED), 0) + 512 * part == sample)
-        ids = ids + dot_nn(conn_t[:, 512 * part : 512 * part + 512], picks)
+    for g in range(groups):
+        ids = ids + jnp.where((sample >> 7) == g, found[16 * g : 16 * g + 16], 0.0)
     ids1 = (ids[0:8] * 256.0 + ids[8:16]).astype(I32)
     live = ids1 > 0
     ids_s[...] = jnp.maximum(ids1 - 1, 0)
@@ -451,7 +453,7 @@
     return [jnp.broadcast_to(v[:, lane + j : lane + j + 1], (8, 128)) for j in range(8)]
 
 
-def panel(diag, p0, p1, below, ahead):
+def panel(diag, p0, p1, below, ahead, q0, q1):
     sub = iota((8, 128), 0)
     out = [None, None]
     for k in range(8):
@@ -472,7 +474,8 @@
                 below[j] = below[j] - c2 * at[j]
             for j in range(8):
                 ahead[j] = ahead[j] - c2 * rep(c2, j)
-    return out, ahead
+            q0, q1 = q0 - c2 * x0, q1 - c2 * x1
+    return out, ahead, q0, q1
 
 
 def product6(a, b):
@@ -492,7 +495,7 @@
 
 
 def finish_kernel(
-    c_hbm, f_hbm, b_hbm, o_ref, t_ref, A, M, uh, um, gf, gh, gm, bf, o_v, c_ref, f_ref, b_ref, sems, loads
+    c_hbm, f_hbm, b_hbm, o_ref, t_ref, A, M, uh, um, gf, gh, gm, bf, bt, o_v, c_ref, f_ref, b_ref, sems, loads
 ):
     get_c = pltpu.make_async_copy(c_hbm, c_ref, loads.at[0])
     get_f = pltpu.make_async_copy(f_hbm, f_ref, loads.at[1])
@@ -500,6 +503,8 @@
     get_c.start()
     get_f.start()
     get_b.start()
+    get_b.wait()
+    get_f.wait()
     get_c.wait()
     for n, (k, i) in enumerate(BLOCKS):
         A[128 * k : 128 * k + 128, 128 * i : 128 * i + 128] = c_ref[n].reshape(128, 128)
@@ -525,7 +530,7 @@
 
         return run
 
-    def solve(k, r, inv_h, inv_m):
+    def reduce(k, r):
         def run():
             rows = slice(128 * r, 128 * r + 128)
             cols = slice(128 * k, 128 * k + 128)
@@ -535,12 +540,32 @@
                 g = g - dot_nn(gh[rows, done], uh[done, cols])
                 g = g - dot_nn(gh[rows, done], um[done, cols])
                 g = g - dot_nn(gm[rows, done], uh[done, cols])
-            h, m = split2(g)
-            g = dot_nt(h, inv_h) + dot_nt(h, inv_m) + dot_nt(m, inv_h)
+            gf[rows, cols] = g
+
+        return run
+
+    def solve(k, r, inv_h, inv_m):
+        def run():
+            rows = slice(128 * r, 128 * r + 128)
+            cols = slice(128 * k, 128 * k + 128)
+            h, m = split2(gf[rows, cols])
+            g = dot_nt(h, inv_h) + dot_nt(m, inv_h)
+            if inv_m is not None:
+                g = g + dot_nt(h, inv_m)
             gf[rows, cols] = g
             h, m = split2(g)
             gh[rows, cols] = h
             gm[rows, cols] = m
+
+        return run
+
+    def flip(s):
+        def run():
+            b = b_ref[...] if s is None else bf[KROWS * s : KROWS * s + KROWS, :]
+            if s is None:
+                bf[...] = b.astype(F32)
+            else:
+                bt[s] = jnp.concatenate([b, b], 0).T
 
         return run
 
@@ -550,10 +575,8 @@
             cols = slice(128 * k, 128 * k + 128)
             g = gf[rows, cols]
             h = g.astype(BF16).astype(F32)
-            b = bf[rows, :]
-            lhs = jnp.concatenate([b, b], 0).astype(BF16)
             rhs = jnp.concatenate([h, g - h], 0).astype(BF16)
-            o_v[s, :, cols] = dot_tn(lhs, rhs)
+            o_v[s, :, cols] = dot_nn(bt[s].astype(BF16), rhs)
 
         return run
 
@@ -561,52 +584,48 @@
         cols = pl.ds(128 * k, 128)
         return pltpu.make_async_copy(o_v.at[:, :, cols], o_ref.at[:, :, cols], sems.at[k])
 
-    fill = []
+    fill = [flip(None)] + [flip(s) for s in range(CAP)] + [reduce(0, r) for r in range(3)]
     for k in range(4):
         lo = 128 * k
         M[:, 0:128] = A[lo : lo + 128, lo : lo + 128]
         M[:, 128:256] = eye
         per = -(-len(fill) // 16)
         diag = spread_cols(M[0:8, 0:128], 0)
+        p0, p1 = M[0:8, 0:128], M[0:8, 128:256]
         for p in range(16):
             top = 8 * p
-            below = ahead = None
+            below = ahead = q0 = q1 = None
             if p < 15:
-                under = M[top + 8 : top + 16, 0:128]
-                below, ahead = spread_cols(under, top), spread_cols(under, top + 8)
-            (u0, u1), diag = panel(
-                diag, M[top : top + 8, 0:128], M[top : top + 8, 128:256], below, ahead
-            )
+                q0, q1 = M[top + 8 : top + 16, 0:128], M[top + 8 : top + 16, 128:256]
+                below, ahead = spread_cols(q0, top), spread_cols(q0, top + 8)
+            (u0, u1), diag, p0, p1 = panel(diag, p0, p1, below, ahead, q0, q1)
             M[top : top + 8, 0:128] = u0
             M[top : top + 8, 128:256] = u1
-            if p < 15:
+            if p < 14:
                 h0, m0, l0 = split3(u0)
                 h1, m1, l1 = split3(u1)
                 lhs = jnp.concatenate([h0, h0, m0, m0, h0, l0], 0).astype(BF16)
                 r0 = jnp.concatenate([h0, m0, h0, m0, l0, h0], 0)
                 r1 = jnp.concatenate([h1, m1, h1, m1, l1, h1], 0)
-                upd = dot_tn(lhs, jnp.concatenate([r0, r1], 1).astype(BF16))
-                if p < 12:
-                    M[top + 8 :, :] = M[top + 8 :, :] - upd[top + 8 :, :]
-                else:
-                    later = iota((32, 256), 0) + 96 >= top + 8
-                    M[96:, :] = M[96:, :] - jnp.where(later, upd[96:, :], 0.0)
+                start = min((top + 16) // 16 * 16, 96)
+                upd = dot_nn(lhs.T[start:, :], jnp.concatenate([r0, r1], 1).astype(BF16))
+                if start < top + 8:
+                    upd = jnp.where(iota((128 - start, 256), 0) + start >= top + 16, upd, 0.0)
+                M[start:, :] = M[start:, :] - upd
             for job in fill[per * p : per * p + per]:
                 job()
         inv = M[:, 128:256]
         A[lo : lo + 128, lo : lo + 128] = jnp.where(upper, M[:, 0:128], 0.0)
         inv_h, inv_m = split2(inv)
         fill = []
-        if k == 0:
-            get_f.wait()
-            get_b.wait()
-            bf[...] = b_ref[...].astype(F32)
         if k < 3:
             across(k, k + 1, inv)()
             trail(k, k + 1, k + 1)()
             fill += [across(k, i, inv) for i in range(k + 2, 4)]
             fill += [trail(k, i, j) for i in range(k + 1, 4) for j in range(i, 4) if j > k + 1]
         fill += [solve(k, r, inv_h, inv_m) for r in range(3)]
+        if k < 3:
+            fill += [reduce(k + 1, r) for r in range(3)]
         fill += [apply(k, s) for s in range(CAP)]
         fill.append(store(k).start)
     for job in fill:
@@ -639,6 +658,7 @@
             pltpu.VMEM((rows, COLS), BF16),
             pltpu.VMEM((rows, COLS), BF16),
             pltpu.VMEM((rows, BAND), F32),
+            pltpu.VMEM((CAP, BAND, 2 * KROWS), F32),
             pltpu.VMEM((CAP, BAND, COLS), F32),
             pltpu.VMEM((10, 16, 8, 128), F32),
             pltpu.VMEM((rows, COLS), BF16),

time: 70.2 us -> 67.7 us (0.964)
  Pallas kernels: 69.2 us -> 66.8 us
    pallas_call x1, Pallas kernels: 19.4 us -> 17 us  [finish(): pl.pallas_call(finish_kernel, out_shape=(jax.ShapeDtypeStruct((CAP, BAND,...]
where the time goes in v5:
time: 67.7 us; the launch traced here: 67.6 us
  Pallas kernels  66.8 us (99%)
  between operations  0.8 us (1%)
    pallas_call x1, Pallas kernels, panel_call(): pl.pallas_call(panel_kernel, out_shape=(jax.ShapeDtypeStruct((160, 8, 128...  49.8 us
    pallas_call x1, Pallas kernels, finish(): pl.pallas_call(finish_kernel, out_shape=(jax.ShapeDtypeStruct((CAP, BAND,...  17 us

profile of v5, /device:TPU:1, one launch (start us, length us, event | category | flops | bytes accessed | tf_op | source)
XLA Modules:
  0.0 67.6 jit_solution(16077821973128615723)
XLA Ops:
  0.6 49.8 %panel_exchange.1 = (f32[160,8,128]{2,1,0:T(8,128)}, bf16[384,512]{1,0:T(8,128)(2,1)}, bf16[384,128]{1,0:T(8,128)(2,1)}) custom-call(s32[1,512]{1,0:T(1,128)} %bitcast.12, s32[8,2048]{1,0:T(8,128)} %bitcast.10, s32[512,128]{1,0:T(8,128)} %bitcast.8, s32[1,512]{1,0:T(1,128)} %bitcast.13, bf16[8,512]{1,0:T(8,128)(2,1)} %bitcast.11, bf16[384,24]{1,0:T(8,128)(2,1)} %bitcast.9, ...), custom_call_target="tpu_custom_call" | custom-call | tf_op jit(solution)/shard_map/panel_exchange/pallas_call | solution.py:396
  50.4 17.0 %factor_and_apply.1 = (f32[16,128,512]{2,1,0:T(8,128)}, f32[8,512]{1,0:T(8,128)}) custom-call(f32[10,16,8,128]{3,2,1,0:T(8,128)} %bitcast.7, bf16[384,512]{1,0:T(8,128)(2,1)} %get-tuple-element.6.f_hbm, bf16[384,128]{1,0:T(8,128)(2,1)} %get-tuple-element.7.b_hbm), custom_call_target="tpu_custom_call" | custom-call | tf_op jit(solution)/shard_map/factor_and_apply/pallas_call | solution.py:644

commit v6 on v5

--- a/solution.py
+++ b/solution.py
@@ -173,35 +173,50 @@
 
 
 def panel_kernel(
-    sample_ref, conn_ref, slot_ref, dev_ref, coords_ref, stiff_ref, basis_ref,
+    sample_in, conn_in, slot_in, dev_in, coords_in, stiff_in, basis_ref,
     gram_ref, f_ref, band_ref,
+    sample_ref, conn_ref, slot_ref, dev_ref, coords_ref, stiff_ref, in_sems,
     basis_v, ids_s, st_s, tab_s, out_s, inc_s, ct_s, b_s, fc_s, c_ref, rbuf, o_ref, f_v, band_v,
     load_sem, x_send, x_recv, b_send, b_recv,
     rs_send, rs_recv, own_sem, z_send, z_recv, xy_send, xy_recv, c_send, c_recv,
     gram_sem, f_sem, band_sem,
 ):
     load = pltpu.make_async_copy(basis_ref, basis_v, load_sem)
-    load.start()
+    pairs = (
+        (sample_in, sample_ref),
+        (conn_in, conn_ref),
+        (slot_in, slot_ref),
+        (dev_in, dev_ref),
+        (coords_in, coords_ref),
+        (stiff_in, stiff_ref),
+    )
+    gets = [pltpu.make_async_copy(a, b, in_sems.at[i]) for i, (a, b) in enumerate(pairs)]
     e = lax.axis_index("elem")
     x = lax.axis_index("snap")
     y, z, c = e >> 4, (e >> 1) & 7, e & 1
     barrier = pltpu.get_barrier_semaphore()
 
     def greet(j, carry):
-        pl.semaphore_signal(barrier, inc=1, device_id=((e + j) & (N_ELEM - 1), x), device_id_type=MESH)
+        v = j - 63 * (j >> 6)
+        pl.semaphore_signal(barrier, inc=1, device_id=((e + v) & (N_ELEM - 1), x), device_id_type=MESH)
         return carry
-
-    lax.fori_loop(1, N_ELEM, greet, 0)
 
     def greet_x(j, carry):
         x2 = (x + 1 + (j >> 2)) & 3
         y2 = j & 3
         pl.semaphore_signal(
-            barrier, inc=1, device_id=(y2 * 16 + z * 2 + c, x2), device_id_type=MESH
+            barrier, inc=1, device_id=((y2 << 4) + (z << 1) + c, x2), device_id_type=MESH
         )
         return carry
 
+    lax.fori_loop(32, 48, greet, 0)
     lax.fori_loop(0, 12, greet_x, 0)
+    lax.fori_loop(48, 95, greet, 0)
+    for get in gets:
+        get.start()
+    load.start()
+    for get in gets:
+        get.wait()
     select, place = index_tables(sample_ref, conn_ref, slot_ref, dev_ref, ids_s, st_s, tab_s)
     load.wait()
     out_s[...] = dot_nn(select, basis_v[...]).astype(BF16).reshape(N_ELEM, 2, NDOF * MODES)
@@ -390,7 +405,6 @@
 
 def panel_call(sample, conn, slots, dev, coords, stiff, basis):
     dma = pltpu.SemaphoreType.DMA
-    vm = pl.BlockSpec(memory_space=pltpu.VMEM)
     n = CAP * KROWS
     width = NDOF * MODES
     return pl.pallas_call(
@@ -400,9 +414,16 @@
             jax.ShapeDtypeStruct((n, COLS), BF16),
             jax.ShapeDtypeStruct((n, BAND), BF16),
         ),
-        in_specs=[vm] * 6 + [pl.BlockSpec(memory_space=pl.ANY)],
+        in_specs=[pl.BlockSpec(memory_space=pl.ANY)] * 7,
         out_specs=(pl.BlockSpec(memory_space=pl.ANY),) * 3,
         scratch_shapes=[
+            pltpu.VMEM((1, SAMPLED), I32),
+            pltpu.VMEM((ENODES, 2048), I32),
+            pltpu.VMEM((512, 128), I32),
+            pltpu.VMEM((1, SAMPLED), I32),
+            pltpu.VMEM((8, MODES), BF16),
+            pltpu.VMEM((16 * KROWS, KROWS), BF16),
+            dma((6,)),
             pltpu.VMEM((NODE_DEV, width), BF16),
             pltpu.VMEM((ENODES, SAMPLED), I32),
             pltpu.VMEM((ENODES, SAMPLED), I32),
@@ -497,19 +518,30 @@
 def finish_kernel(
     c_hbm, f_hbm, b_hbm, o_ref, t_ref, A, M, uh, um, gf, gh, gm, bf, bt, o_v, c_ref, f_ref, b_ref, sems, loads
 ):
-    get_c = pltpu.make_async_copy(c_hbm, c_ref, loads.at[0])
+    get_c0 = pltpu.make_async_copy(c_hbm.at[pl.ds(0, 1)], c_ref.at[pl.ds(0, 1)], loads.at[3])
+    get_c = pltpu.make_async_copy(c_hbm.at[pl.ds(1, 9)], c_ref.at[pl.ds(1, 9)], loads.at[0])
     get_f = pltpu.make_async_copy(f_hbm, f_ref, loads.at[1])
     get_b = pltpu.make_async_copy(b_hbm, b_ref, loads.at[2])
+    get_c0.start()
     get_c.start()
     get_f.start()
     get_b.start()
-    get_b.wait()
-    get_f.wait()
-    get_c.wait()
-    for n, (k, i) in enumerate(BLOCKS):
-        A[128 * k : 128 * k + 128, 128 * i : 128 * i + 128] = c_ref[n].reshape(128, 128)
-    for k in range(1, 4):
-        A[128 * k : 128 * k + 128, 0 : 128 * k] = jnp.zeros((128, 128 * k), F32)
+    get_c0.wait()
+    A[0:128, 0:128] = c_ref[0].reshape(128, 128)
+
+    def rest():
+        get_b.wait()
+        get_f.wait()
+        get_c.wait()
+
+    def unpack(n, k, i):
+        def run():
+            A[128 * k : 128 * k + 128, 128 * i : 128 * i + 128] = c_ref[n].reshape(128, 128)
+            if i > k:
+                A[128 * i : 128 * i + 128, 128 * k : 128 * k + 128] = jnp.zeros((128, 128), F32)
+
+        return run
+
     eye = jnp.where(iota((128, 128), 0) == iota((128, 128), 1), 1.0, 0.0)
     upper = iota((128, 128), 0) <= iota((128, 128), 1)
 
@@ -584,7 +616,8 @@
         cols = pl.ds(128 * k, 128)
         return pltpu.make_async_copy(o_v.at[:, :, cols], o_ref.at[:, :, cols], sems.at[k])
 
-    fill = [flip(None)] + [flip(s) for s in range(CAP)] + [reduce(0, r) for r in range(3)]
+    fill = [rest] + [unpack(n, k, i) for n, (k, i) in enumerate(BLOCKS) if n]
+    fill += [flip(None)] + [flip(s) for s in range(CAP)] + [reduce(0, r) for r in range(3)]
     for k in range(4):
         lo = 128 * k
         M[:, 0:128] = A[lo : lo + 128, lo : lo + 128]
@@ -664,7 +697,7 @@
             pltpu.VMEM((rows, COLS), BF16),
             pltpu.VMEM((rows, BAND), BF16),
             pltpu.SemaphoreType.DMA((4,)),
-            pltpu.SemaphoreType.DMA((3,)),
+            pltpu.SemaphoreType.DMA((4,)),
         ],
         name="factor_and_apply",
     )(gram, forces, band)

time: 67.7 us -> 67.4 us (level)
  no operation moved by 1% of the time
where the time goes in v6:
time: 67.4 us; the launch traced here: 67.3 us
  Pallas kernels  66.5 us (99%)
  between operations  0.8 us (1%)
    pallas_call x1, Pallas kernels, panel_call(): pl.pallas_call(panel_kernel, out_shape=(jax.ShapeDtypeStruct((160, 8, 128...  49.8 us
    pallas_call x1, Pallas kernels, finish(): pl.pallas_call(finish_kernel, out_shape=(jax.ShapeDtypeStruct((CAP, BAND,...  16.7 us

profile of v6, /device:TPU:1, one launch (start us, length us, event | category | flops | bytes accessed | tf_op | source)
XLA Modules:
  0.0 67.3 jit_solution(16949887096956533099)
XLA Ops:
  0.6 49.8 %panel_exchange.1 = (f32[160,8,128]{2,1,0:T(8,128)}, bf16[384,512]{1,0:T(8,128)(2,1)}, bf16[384,128]{1,0:T(8,128)(2,1)}) custom-call(s32[1,512]{1,0:T(1,128)} %bitcast.12, s32[8,2048]{1,0:T(8,128)} %bitcast.10, s32[512,128]{1,0:T(8,128)} %bitcast.8, s32[1,512]{1,0:T(1,128)} %bitcast.13, bf16[8,512]{1,0:T(8,128)(2,1)} %bitcast.11, bf16[384,24]{1,0:T(8,128)(2,1)} %bitcast.9, ...), custom_call_target="tpu_custom_call" | custom-call | tf_op jit(solution)/shard_map/panel_exchange/pallas_call | solution.py:410
  50.4 16.7 %factor_and_apply.1 = (f32[16,128,512]{2,1,0:T(8,128)}, f32[8,512]{1,0:T(8,128)}) custom-call(f32[10,16,8,128]{3,2,1,0:T(8,128)} %bitcast.7, bf16[384,512]{1,0:T(8,128)(2,1)} %get-tuple-element.6.f_hbm, bf16[384,128]{1,0:T(8,128)(2,1)} %get-tuple-element.7.b_hbm), custom_call_target="tpu_custom_call" | custom-call | tf_op jit(solution)/shard_map/factor_and_apply/pallas_call | solution.py:677

commit v7 on v6

--- a/solution.py
+++ b/solution.py
@@ -326,7 +326,8 @@
         def _():
             pltpu.make_async_copy(o_ref.at[at], o_ref.at[at], z_recv.at[k]).wait()
 
-        def send_tile(j, carry):
+        def send_tile(i, carry):
+            j = i - 15 * (i >> 4)
             x2, y2 = (x + (j >> 2)) & 3, (y + j) & 3
             pltpu.make_async_remote_copy(
                 src_ref=o_ref.at[at],
@@ -338,7 +339,7 @@
             ).start()
             return carry
 
-        lax.fori_loop(1, 16, send_tile, 0)
+        lax.fori_loop(10, 25, send_tile, 0)
 
     def core_copy(j):
         x2, y2 = (x + (j >> 2)) & 3, (y + j) & 3
@@ -612,9 +613,11 @@
 
         return run
 
-    def store(k):
+    def store(k, part=None):
         cols = pl.ds(128 * k, 128)
-        return pltpu.make_async_copy(o_v.at[:, :, cols], o_ref.at[:, :, cols], sems.at[k])
+        some = pl.ds(0, CAP) if part is None else pl.ds(4 * part, 4)
+        sem = sems.at[k if part is None else k + part]
+        return pltpu.make_async_copy(o_v.at[some, :, cols], o_ref.at[some, :, cols], sem)
 
     fill = [rest] + [unpack(n, k, i) for n, (k, i) in enumerate(BLOCKS) if n]
     fill += [flip(None)] + [flip(s) for s in range(CAP)] + [reduce(0, r) for r in range(3)]
@@ -659,15 +662,21 @@
         fill += [solve(k, r, inv_h, inv_m) for r in range(3)]
         if k < 3:
             fill += [reduce(k + 1, r) for r in range(3)]
-        fill += [apply(k, s) for s in range(CAP)]
-        fill.append(store(k).start)
+            fill += [apply(k, s) for s in range(CAP)]
+            fill.append(store(k).start)
+        else:
+            for part in range(4):
+                fill += [apply(k, s) for s in range(4 * part, 4 * part + 4)]
+                fill.append(store(k, part).start)
     for job in fill:
         job()
     share = COLS // N_ELEM
     start = pl.multiple_of(lax.axis_index("elem") * share, share)
     t_ref[...] = A[pl.ds(start, share), :]
-    for k in range(4):
+    for k in range(3):
         store(k).wait()
+    for part in range(4):
+        store(3, part).wait()
 
 
 def finish(gram, forces, band):
@@ -696,7 +705,7 @@
             pltpu.VMEM((10, 16, 8, 128), F32),
             pltpu.VMEM((rows, COLS), BF16),
             pltpu.VMEM((rows, BAND), BF16),
-            pltpu.SemaphoreType.DMA((4,)),
+            pltpu.SemaphoreType.DMA((7,)),
             pltpu.SemaphoreType.DMA((4,)),
         ],
         name="factor_and_apply",

time: 67.4 us -> 67.4 us (level)
  no operation moved by 1% of the time
where the time goes in v7:
time: 67.4 us; the launch traced here: 67.3 us
  Pallas kernels  66.5 us (99%)
  between operations  0.8 us (1%)
    pallas_call x1, Pallas kernels, panel_call(): pl.pallas_call(panel_kernel, out_shape=(jax.ShapeDtypeStruct((160, 8, 128...  49.9 us
    pallas_call x1, Pallas kernels, finish(): pl.pallas_call(finish_kernel, out_shape=(jax.ShapeDtypeStruct((CAP, BAND,...  16.6 us

profile of v7, /device:TPU:1, one launch (start us, length us, event | category | flops | bytes accessed | tf_op | source)
XLA Modules:
  0.0 67.3 jit_solution(16601179774647265694)
XLA Ops:
  0.6 49.9 %panel_exchange.1 = (f32[160,8,128]{2,1,0:T(8,128)}, bf16[384,512]{1,0:T(8,128)(2,1)}, bf16[384,128]{1,0:T(8,128)(2,1)}) custom-call(s32[1,512]{1,0:T(1,128)} %bitcast.12, s32[8,2048]{1,0:T(8,128)} %bitcast.10, s32[512,128]{1,0:T(8,128)} %bitcast.8, s32[1,512]{1,0:T(1,128)} %bitcast.13, bf16[8,512]{1,0:T(8,128)(2,1)} %bitcast.11, bf16[384,24]{1,0:T(8,128)(2,1)} %bitcast.9, ...), custom_call_target="tpu_custom_call" | custom-call | tf_op jit(solution)/shard_map/panel_exchange/pallas_call | solution.py:411
  50.5 16.6 %factor_and_apply.1 = (f32[16,128,512]{2,1,0:T(8,128)}, f32[8,512]{1,0:T(8,128)}) custom-call(f32[10,16,8,128]{3,2,1,0:T(8,128)} %bitcast.7, bf16[384,512]{1,0:T(8,128)(2,1)} %get-tuple-element.6.f_hbm, bf16[384,128]{1,0:T(8,128)(2,1)} %get-tuple-element.7.b_hbm), custom_call_target="tpu_custom_call" | custom-call | tf_op jit(solution)/shard_map/factor_and_apply/pallas_call | solution.py:686
